TPU v7x, 256 devices: a whole 4x4x8 slice. The times are simulated.
256 devices in a mesh: samp: 16 (over y_hi, x, core), head: 16 (over y_lo, z).
Axes of the slice: x: 4, y: 4 (y_hi: 2, y_lo: 2; y = y_hi * 2 + y_lo), z: 8, core: 2. Of those that a mesh axis runs over, the one named last changes fastest.
Arguments:
- input_tokens: bfloat16 [32, 512, 768], P('samp'), may hold values from -6 to 6
- output_cotangent: bfloat16 [32, 512, 768], P('samp'), may hold values from -15 to 15
- query_weight: bfloat16 [768, 768], P(None, 'head'), may hold values from -0.21875 to 0.21875
- key_weight: bfloat16 [768, 768], P(None, 'head'), may hold values from -0.21875 to 0.21875
- value_weight: bfloat16 [768, 768], P(None, 'head'), may hold values from -0.21875 to 0.21875
- output_weight: bfloat16 [768, 768], P('head'), may hold values from -0.21875 to 0.21875
- pair_bias: bfloat16 [16, 512, 512], P('head'), may hold values from -6 to 240
- valid_len: int32 [1], replicated, may hold values from 256 to 512
- pair_in: bfloat16 [512, 512, 128], P('head', 'samp'), may hold values from -6 to 6
- w_bias: bfloat16 [128, 16], replicated, may hold values from -6 to 6
- t_gate: bfloat16 [2, 128, 256], replicated, may hold values from -0.5 to 0.5
- t_up: bfloat16 [2, 128, 256], replicated, may hold values from -0.5 to 0.5
- t_down: bfloat16 [2, 256, 128], replicated, may hold values from -0.375 to 0.375
Outputs:
- d_tokens: bfloat16 [32, 512, 768], P('samp', None, 'head')
- d_pair: bfloat16 [512, 512, 128], P('head', 'samp')
- d_trans_gate: float32 [2, 128, 256], replicated
- d_trans_up: float32 [2, 128, 256], replicated
- d_trans_down: float32 [2, 256, 128], replicated
All inputs are finite; a program needn't handle non-finite values.
Results may differ from a plain program's by a relative error of at most 0.02.
Values may be sent and summed in bfloat16 or wider, within the bound.
No kernel may reach another device: no remote copies, remote signals or barrier semaphores. Data moves between devices by JAX's collectives and lax.ppermute only.
A program may use at most 64 MiB of HBM per device.

v0:
```python
import math

import jax
import jax.numpy as jnp
from jax import lax
from jax.sharding import Mesh
from jax.sharding import PartitionSpec as P

HD = 48
HEAD = ("head_0", "head_1")
SAMP_HEAD = ("samp", "head_0", "head_1")


EPS_NORM = 1e-05
MASKED = -1e30


def sum_in_order(pieces, axes, turns):
    inside = pieces.shape[1:]
    pieces = pieces.reshape(*(lax.axis_size(a) for a in axes), *inside)
    pieces = jnp.moveaxis(pieces, turns, range(len(axes))).reshape(-1, *inside)
    for k in turns:
        pieces = lax.psum_scatter(pieces, axes[k], scatter_dimension=0, tiled=True)
    return pieces[0]


def cut_along(array, dim, length):
    dims = array.shape
    pieces = array.reshape(*dims[:dim], length, dims[dim] // length, *dims[dim + 1 :])
    return jnp.moveaxis(pieces, dim, 0)


def scatter_axes(array, axes, turns, dim):
    length = lax.axis_size(axes)
    return sum_in_order(cut_along(array, dim, length), axes, turns)


def sent_and_summed(array, axis, dim):
    length = lax.axis_size(axis)
    pieces = lax.all_to_all(cut_along(array, dim, length), axis, 0, 0, tiled=True)
    return jnp.sum(pieces.astype(jnp.float32), axis=0)


def in_one(arrays, axis):
    ravelled, at, gathered = (jnp.concatenate([a.reshape(-1) for a in arrays]), 0, [])
    total = lax.psum(ravelled, axis)
    for a in arrays:
        gathered.append(total[at : at + a.size].reshape(a.shape))
        at += a.size
    return tuple(gathered)


def layer_forward(field, gate_weight, up_weight, down_weight):
    centred = field - jnp.mean(field, axis=-1, keepdims=True)
    variance = jnp.mean(centred * centred, axis=-1, keepdims=True)
    inv_std = lax.rsqrt(variance + EPS_NORM)
    normed = centred * inv_std
    normed_low = normed.astype(jnp.bfloat16)
    gate_proj = jnp.dot(normed_low, gate_weight, preferred_element_type=jnp.float32)
    up_proj = jnp.dot(normed_low, up_weight, preferred_element_type=jnp.float32)
    sigmoid_gate = jax.nn.sigmoid(gate_proj)
    hidden = (gate_proj * sigmoid_gate * up_proj).astype(jnp.bfloat16)
    result = field + jnp.dot(hidden, down_weight, preferred_element_type=jnp.float32)
    return (result, (normed, normed_low, inv_std, gate_proj, up_proj, sigmoid_gate, hidden))


def layer_backward(grad_next, saved, gate_weight, up_weight, down_weight):
    normed, normed_low, inv_std, gate_proj, up_proj, sigmoid_gate, hidden = saved
    grad_low = grad_next.astype(jnp.bfloat16)
    down_sum = jnp.dot(hidden.T, grad_low, preferred_element_type=jnp.float32)
    grad_hidden = jnp.dot(grad_low, down_weight.T, preferred_element_type=jnp.float32)
    grad_gate = (
        grad_hidden * up_proj * sigmoid_gate * (1.0 + gate_proj * (1.0 - sigmoid_gate))
    ).astype(jnp.bfloat16)
    grad_up = (grad_hidden * gate_proj * sigmoid_gate).astype(jnp.bfloat16)
    gate_sum = jnp.dot(normed_low.T, grad_gate, preferred_element_type=jnp.float32)
    up_sum = jnp.dot(normed_low.T, grad_up, preferred_element_type=jnp.float32)
    grad_normed = jnp.dot(grad_gate, gate_weight.T, preferred_element_type=jnp.float32) + jnp.dot(
        grad_up, up_weight.T, preferred_element_type=jnp.float32
    )
    inner = inv_std * (
        grad_normed
        - jnp.mean(grad_normed, axis=-1, keepdims=True)
        - normed * jnp.mean(grad_normed * normed, axis=-1, keepdims=True)
    )
    return (grad_next + inner, gate_sum, up_sum, down_sum)


def pair_block(pair_low, grad_top, t_gate, t_up, t_down):
    field = pair_low.astype(jnp.float32)
    saved_list = []
    for layer in range(t_gate.shape[0]):
        field, saved = layer_forward(field, t_gate[layer], t_up[layer], t_down[layer])
        saved_list.append(saved)
    grad_field = grad_top
    gate_list, up_list, down_list = ([], [], [])
    for layer in reversed(range(t_gate.shape[0])):
        grad_field, gate_sum, up_sum, down_sum = layer_backward(
            grad_field, saved_list[layer], t_gate[layer], t_up[layer], t_down[layer]
        )
        gate_list.insert(0, gate_sum)
        up_list.insert(0, up_sum)
        down_list.insert(0, down_sum)
    return (grad_field, jnp.stack(gate_list), jnp.stack(up_list), jnp.stack(down_list))


def per_device(
    input_tokens,
    output_cotangent,
    query_weight,
    key_weight,
    value_weight,
    output_weight,
    pair_bias,
    valid_len,
    pair_in,
    w_bias,
    t_gate,
    t_up,
    t_down,
):
    samples = input_tokens.shape[0]
    tokens = input_tokens.shape[1]
    local_width = query_weight.shape[1]
    local_heads = local_width // HD
    score_scale = 1.0 / math.sqrt(HD)
    kept_keys = jnp.arange(tokens, dtype=jnp.int32) < valid_len[0]
    inner_weight = jnp.concatenate([query_weight, key_weight, value_weight], axis=1)
    projected = jnp.einsum(
        "tvz,zl->tvl", input_tokens, inner_weight, preferred_element_type=jnp.float32
    ).astype(jnp.bfloat16)
    attention_gradient = jnp.einsum(
        "cjy,hy->cjh", output_cotangent, output_weight, preferred_element_type=jnp.float32
    ).astype(jnp.bfloat16)
    split_heads = projected.reshape(samples, tokens, 3, local_heads, HD).transpose(2, 3, 0, 1, 4)
    attn_heads = attention_gradient.reshape(samples, tokens, local_heads, HD).transpose(2, 0, 1, 3)

    def attend_head(inputs):
        query, keys, values, grad_out, bias_block = inputs
        scores = (
            jnp.einsum("sie,sje->sij", query, keys, preferred_element_type=jnp.float32)
            * score_scale
            + bias_block.astype(jnp.float32)[None]
        )
        scores = jnp.where(kept_keys[None, None, :], scores, MASKED)
        row_max = jnp.max(scores, axis=-1, keepdims=True)
        exp_scores = jnp.exp(scores - row_max)
        attn_probs = exp_scores / jnp.sum(exp_scores, axis=-1, keepdims=True)
        probs_low = attn_probs.astype(jnp.bfloat16)
        grad_probs = jnp.einsum(
            "sie,sje->sij", grad_out, values, preferred_element_type=jnp.float32
        )
        grad_scores = attn_probs * (
            grad_probs - jnp.sum(attn_probs * grad_probs, axis=-1, keepdims=True)
        )
        scores_low = grad_scores.astype(jnp.bfloat16)
        value_partial_gradient = jnp.sum(grad_scores, axis=0)
        grad_query = (
            jnp.einsum("sij,sje->sie", scores_low, keys, preferred_element_type=jnp.float32)
            * score_scale
        ).astype(jnp.bfloat16)
        grad_key = (
            jnp.einsum("sij,sie->sje", scores_low, query, preferred_element_type=jnp.float32)
            * score_scale
        ).astype(jnp.bfloat16)
        grad_value = jnp.einsum(
            "sij,sie->sje", probs_low, grad_out, preferred_element_type=jnp.float32
        ).astype(jnp.bfloat16)
        return (grad_query, grad_key, grad_value, value_partial_gradient)

    head_outs = lax.map(
        attend_head, (split_heads[0], split_heads[1], split_heads[2], attn_heads, pair_bias)
    )
    joined_gradients = jnp.concatenate(
        [
            part_grad.transpose(1, 2, 0, 3).reshape(samples, tokens, local_width)
            for part_grad in head_outs[:3]
        ],
        axis=2,
    )
    token_terms = jnp.einsum(
        "tla,ua->tlu", joined_gradients, inner_weight, preferred_element_type=jnp.float32
    ).astype(jnp.bfloat16)
    d_tokens = scatter_axes(token_terms, HEAD, (1, 0), 2).astype(jnp.float32).astype(jnp.bfloat16)
    bias_parts = head_outs[3].astype(jnp.bfloat16)
    summed = sent_and_summed(bias_parts, "samp", 2)
    owned_grad = lax.all_to_all(
        summed.astype(jnp.bfloat16), HEAD, split_axis=1, concat_axis=0, tiled=True
    )
    pair_rows, pair_cols, channels = pair_in.shape
    grad_top = jnp.einsum("hrc,zh->rcz", owned_grad, w_bias, preferred_element_type=jnp.float32)
    grad_field, gate_sum, up_sum, down_sum = pair_block(
        pair_in.reshape(pair_rows * pair_cols, channels),
        grad_top.reshape(pair_rows * pair_cols, channels),
        t_gate,
        t_up,
        t_down,
    )
    total_gate, total_up, total_down = in_one((gate_sum, up_sum, down_sum), SAMP_HEAD)
    d_pair = grad_field.reshape(pair_rows, pair_cols, channels).astype(jnp.bfloat16)
    return (d_tokens, d_pair, total_gate / tokens, total_up / tokens, total_down / tokens)


def solution(mesh):
    torus = Mesh(mesh.devices.reshape(mesh.shape["samp"], 2, 8), ("samp", "head_0", "head_1"))
    return jax.shard_map(
        per_device,
        mesh=torus,
        in_specs=(
            P("samp", None, None),
            P("samp", None, None),
            P(None, HEAD),
            P(None, HEAD),
            P(None, HEAD),
            P(HEAD, None),
            P(HEAD, None, None),
            P(),
            P(HEAD, "samp", None),
            P(),
            P(),
            P(),
            P(),
        ),
        out_specs=(P("samp", None, HEAD), P(HEAD, "samp", None), P(), P(), P()),
        check_vma=False,
    )
```

profile of v0, /device:TPU:2, one launch (start us, length us, event | category | flops | bytes accessed | tf_op | source)
XLA Modules:
  0.0 339.2 jit_solution(6025551784304046151)
XLA Ops:
  8.1 1.3 bitcast_convert_fusion
  9.4 1.3 copy.47
  11.6 0.6 convolution_convert_fusion.1
  12.3 0.6 convolution_convert_fusion.3
  12.9 2.3 fusion.65
  15.2 1.1 convolution_convert_fusion.2
  16.3 2.2 multiply_reduce_fusion
  18.6 1.5 fusion.9
  20.0 0.4 fusion.2
  20.5 0.3 fusion.3
  20.7 1.8 convolution_convert_fusion
  22.5 1.7 copy.51
  24.3 1.3 copy.52
  25.6 7.6 %all-to-all-start = ((bf16[16,1,512,32]{2,3,1,0:T(8,128)(2,1)}), bf16[16,1,512,32]{2,3,1,0:T(8,128)(2,1)}, u32[]{:S(2)}, u32[]{:S(2)}) async-start(bf16[16,1,512,32]{2,3,1,0:T(8,128)(2,1)} %bitcast.173), calls=%async_computation.2 | async-start | bytes 1048576 | tf_op jit(solution)/shard_map/all_to_all | solution.py:40
  33.5 0.4 multiply_reduce_fusion.4
  33.9 0.3 multiply_convert_fusion.6
  34.5 1.3 multiply_convert_fusion.5
  35.8 0.4 fusion.66
  36.3 0.4 multiply_reduce_fusion.3
  36.7 0.3 fusion.13
  37.0 1.3 fusion.32
  38.3 3.7 %all-to-all-done = bf16[16,1,512,32]{2,3,1,0:T(8,128)(2,1)} async-done(((bf16[16,1,512,32]{2,3,1,0:T(8,128)(2,1)}), bf16[16,1,512,32]{2,3,1,0:T(8,128)(2,1)}, u32[]{:S(2)}, u32[]{:S(2)}) %all-to-all-start) | async-done | bytes 524320 | tf_op jit(solution)/shard_map/all_to_all | solution.py:40
  42.0 1.1 bitcast_reduce_fusion
  43.3 0.5 broadcast.157
  43.8 1.4 reduce.4
  45.2 0.8 reshape.197
  46.0 8.8 %all-to-all-start.1 = ((bf16[16,2,512]{2,1,0:T(2,128)(2,1)}), bf16[16,2,512]{2,1,0:T(2,128)(2,1)S(1)}, u32[]{:S(2)}, u32[]{:S(2)}) async-start(bf16[16,2,512]{2,1,0:T(2,128)(2,1)} %reshape.197), calls=%async_computation.3 | async-start | bytes 65536 | tf_op jit(solution)/shard_map/all_to_all | solution.py:187
  55.1 2.1 fusion.35
  57.3 0.8 rsqrt.22
  58.1 5.3 %all-to-all-done.1 = bf16[16,2,512]{2,1,0:T(2,128)(2,1)S(1)} async-done(((bf16[16,2,512]{2,1,0:T(2,128)(2,1)}), bf16[16,2,512]{2,1,0:T(2,128)(2,1)S(1)}, u32[]{:S(2)}, u32[]{:S(2)}) %all-to-all-start.1) | async-done | bytes 32800 | tf_op jit(solution)/shard_map/all_to_all | solution.py:187
  64.4 2.2 multiply_convert_fusion.3
  66.7 0.3 fusion.30
  67.6 0.7 fusion.64
  68.3 0.6 multiply_add_fusion
  68.9 0.3 convolution_bitcast_fusion.1
  69.5 0.4 copy-done.25
  69.8 0.6 multiply_convert_fusion.1
  70.7 0.7 fusion.63
  71.4 1.3 fusion.12
  73.6 0.3 copy-done.4
  74.0 0.3 copy-done.5
  74.3 0.5 convolution_bitcast_fusion
  74.8 0.9 pad_maximum_fusion
  75.8 0.7 reduce-scatter.5.cloned.1.call-update
  76.5 251.8 %all-reduce.2.cloned.1.call-done = f32[196608]{0:T(1024)} async-done(((f32[196608]{0:T(1024)}), f32[196608]{0:T(1024)}) %all-reduce.2.cloned.1.call-update) | async-done | bytes 786448 | tf_op jit(solution)/shard_map/psum | solution.py:46
  328.3 1.9 slice_multiply_fusion
  330.2 0.8 div.74
  330.9 0.8 div.76
  (85 shorter events, 4.2 us)
Async XLA Ops:
  8.0 3.5 %copy-start = (bf16[2,512,768]{2,1,0:T(8,128)(2,1)S(1)}, bf16[2,512,768]{2,1,0:T(8,128)(2,1)}, u32[]{:S(2)}) copy-start(bf16[2,512,768]{2,1,0:T(8,128)(2,1)} %param.13) | copy-start | bytes 4718596
  8.0 3.5 %copy-start.22 = (bf16[768,48]{0,1:T(8,128)(2,1)S(1)}, bf16[768,48]{0,1:T(8,128)(2,1)}, u32[]{:S(2)}) copy-start(bf16[768,48]{0,1:T(8,128)(2,1)} %param.17) | copy-start | bytes 221188
  8.0 3.5 %copy-start.23 = (bf16[768,48]{0,1:T(8,128)(2,1)S(1)}, bf16[768,48]{0,1:T(8,128)(2,1)}, u32[]{:S(2)}) copy-start(bf16[768,48]{0,1:T(8,128)(2,1)} %param.16) | copy-start | bytes 221188
  8.0 3.5 %copy-start.24 = (bf16[768,48]{0,1:T(8,128)(2,1)S(1)}, bf16[768,48]{0,1:T(8,128)(2,1)}, u32[]{:S(2)}) copy-start(bf16[768,48]{0,1:T(8,128)(2,1)} %param.15) | copy-start | bytes 221188
  8.0 67.8 %reduce-scatter.3.cloned.1.call-start = ((), (), s32[]{:S(2)}) async-start(), calls=%async_computation.4 | async-start | bytes 1769472 | tf_op jit(solution)/shard_map/reduce_scatter | solution.py:23
  9.4 2.9 copy-start.16
  10.7 1.5 copy-start.3
  11.5 1.3 copy-start.8
  16.3 2.3 copy-start.2
  25.6 7.7 %copy-start.1 = (bf16[32,32,128]{2,1,0:T(8,128)(2,1)S(1)}, bf16[32,32,128]{2,1,0:T(8,128)(2,1)}, u32[]{:S(2)}) copy-start(bf16[32,32,128]{2,1,0:T(8,128)(2,1)} %param.21) | copy-start | bytes 786436
  25.6 8.6 %copy-start.9 = (bf16[2,128,256]{2,1,0:T(8,128)(2,1)S(1)}, bf16[2,128,256]{2,1,0:T(8,128)(2,1)}, u32[]{:S(2)}) copy-start(bf16[2,128,256]{2,1,0:T(8,128)(2,1)} %param.23) | copy-start | bytes 393220
  25.6 8.9 %copy-start.11 = (bf16[2,128,256]{2,1,0:T(8,128)(2,1)S(1)}, bf16[2,128,256]{2,1,0:T(8,128)(2,1)}, u32[]{:S(2)}) copy-start(bf16[2,128,256]{2,1,0:T(8,128)(2,1)} %param.24) | copy-start | bytes 393220
  25.6 16.4 %all-to-all-start = ((bf16[16,1,512,32]{2,3,1,0:T(8,128)(2,1)}), bf16[16,1,512,32]{2,3,1,0:T(8,128)(2,1)}, u32[]{:S(2)}, u32[]{:S(2)}) async-start(bf16[16,1,512,32]{2,3,1,0:T(8,128)(2,1)} %bitcast.173), calls=%async_computation.2 | async-start | bytes 1048576 | tf_op jit(solution)/shard_map/all_to_all | solution.py:40
  33.8 2.0 copy-start.13
  34.5 1.3 copy-start.6
  34.5 1.3 copy-start.19
  36.3 6.8 %copy-start.14 = (f32[1024]{0:T(1024)}, f32[1024]{0:T(1024)S(1)}, u32[]{:S(2)}) copy-start(f32[1024]{0:T(1024)S(1)} %broadcast_multiply_fusion.5) | copy-start | bytes 12292
  36.6 6.5 %copy-start.17 = (f32[1024]{0:T(1024)}, f32[1024]{0:T(1024)S(1)}, u32[]{:S(2)}) copy-start(f32[1024]{0:T(1024)S(1)} %add_rsqrt_fusion.1) | copy-start | bytes 12292
  46.0 18.1 %copy-start.21 = (bf16[128,16]{0,1:T(8,128)(2,1)S(1)}, bf16[128,16]{0,1:T(8,128)(2,1)}, u32[]{:S(2)}) copy-start(bf16[128,16]{0,1:T(8,128)(2,1)} %param.22) | copy-start | bytes 12292
  46.0 17.4 %all-to-all-start.1 = ((bf16[16,2,512]{2,1,0:T(2,128)(2,1)}), bf16[16,2,512]{2,1,0:T(2,128)(2,1)S(1)}, u32[]{:S(2)}, u32[]{:S(2)}) async-start(bf16[16,2,512]{2,1,0:T(2,128)(2,1)} %reshape.197), calls=%async_computation.3 | async-start | bytes 65536 | tf_op jit(solution)/shard_map/all_to_all | solution.py:187
  54.9 273.5 %all-reduce.2.cloned.1.call-start = ((), (), s32[]{:S(2)}) async-start(), calls=%async_computation.6 | async-start | bytes 1572864 | tf_op jit(solution)/shard_map/psum | solution.py:46
  64.4 2.3 copy-start.10
  66.6 0.9 copy-start.12
  66.7 0.9 copy-start.15
  66.7 0.9 copy-start.18
  68.2 1.2 copy-start.7
  68.2 1.2 copy-start.20
  68.3 1.6 copy-start.25
  72.7 1.2 copy-start.4
  72.7 1.5 copy-start.5
  75.7 256.0 %reduce-scatter.5.cloned.1.call-start = ((), (), s32[]{:S(2)}) async-start(), calls=%async_computation.5 | async-start | bytes 294912 | tf_op jit(solution)/shard_map/reduce_scatter | solution.py:23
Sparse Core Ops, SparseCore 0:
  25.7 44.1 reduce-scatter.2
  79.6 12.0 reduce-scatter.4
Sparse Core Ops, SparseCore 1:
  75.8 252.4 all-reduce.1
where the time goes:
time: 340 us; the launch traced here: 339 us
  waiting for transfers between devices  262 us (77%)
  matrix products  21.6 us (6%)
  between operations  16.9 us (5%)
  starting transfers between devices  16.8 us (5%)
  other arithmetic  11.8 us (3%)
  local copies, waits for them, and re-layouts  10.7 us (3%)
    psum x1, waiting for transfers between devices, in_one(): total = lax.psum(ravelled, axis)  252 us
    all_to_all x1, starting transfers between devices, per_device(): lax.all_to_all(summed.astype(jnp.bfloat16), HEAD, split_axis=1, concat_ax...  8.83 us
    all_to_all x1, starting transfers between devices, sent_and_summed(): lax.all_to_all(cut_along(array, dim, length), axis, 0, 0, tiled=True)  7.62 us
  transfers between devices with their start and end apart: 5, of which 3 were waited for; matrix products, arithmetic and copies ran while one was open for 8% of the time, Pallas kernels for 0%

commit v1 on v0

--- a/solution.py
+++ b/solution.py
@@ -7,8 +7,9 @@
 from jax.sharding import PartitionSpec as P
 
 HD = 48
-HEAD = ("head_0", "head_1")
-SAMP_HEAD = ("samp", "head_0", "head_1")
+SAMP = ("yh", "x", "core")
+HEAD = ("yl", "z")
+PLANE = ("yh", "x", "yl")
 
 
 EPS_NORM = 1e-05
@@ -41,9 +42,32 @@
     return jnp.sum(pieces.astype(jnp.float32), axis=0)
 
 
-def in_one(arrays, axis):
-    ravelled, at, gathered = (jnp.concatenate([a.reshape(-1) for a in arrays]), 0, [])
-    total = lax.psum(ravelled, axis)
+def exchange(pieces, axes):
+    return lax.all_to_all(pieces, axes, 0, 0, tiled=True)
+
+
+def summed(pieces):
+    return jnp.sum(pieces.astype(jnp.float32), axis=0)
+
+
+def other_core(array):
+    return lax.ppermute(array, "core", [(0, 1), (1, 0)])
+
+
+def sum_everywhere(arrays):
+    low = jnp.concatenate([a.astype(jnp.bfloat16).reshape(-1) for a in arrays])
+    halves = low.reshape(2, 16, -1, 128)
+    second = lax.axis_index("core") == 1
+    kept = jnp.where(second, halves[1], halves[0])
+    sent = jnp.where(second, halves[0], halves[1])
+    half = (kept.astype(jnp.float32) + other_core(sent).astype(jnp.float32)).astype(jnp.bfloat16)
+    block = summed(exchange(half, PLANE)).astype(jnp.bfloat16)
+    block = summed(exchange(jnp.broadcast_to(block, (8, *block.shape)), "z")).astype(jnp.bfloat16)
+    half = exchange(jnp.broadcast_to(block, (16, *block.shape)), PLANE)
+    other = other_core(half)
+    total = jnp.concatenate([jnp.where(second, other, half), jnp.where(second, half, other)])
+    total = total.astype(jnp.float32).reshape(-1)
+    gathered, at = [], 0
     for a in arrays:
         gathered.append(total[at : at + a.size].reshape(a.shape))
         at += a.size
@@ -183,7 +207,7 @@
     ).astype(jnp.bfloat16)
     d_tokens = scatter_axes(token_terms, HEAD, (1, 0), 2).astype(jnp.float32).astype(jnp.bfloat16)
     bias_parts = head_outs[3].astype(jnp.bfloat16)
-    summed = sent_and_summed(bias_parts, "samp", 2)
+    summed = sent_and_summed(bias_parts, SAMP, 2)
     owned_grad = lax.all_to_all(
         summed.astype(jnp.bfloat16), HEAD, split_axis=1, concat_axis=0, tiled=True
     )
@@ -196,31 +220,33 @@
         t_up,
         t_down,
     )
-    total_gate, total_up, total_down = in_one((gate_sum, up_sum, down_sum), SAMP_HEAD)
+    total_gate, total_up, total_down = sum_everywhere(
+        (gate_sum / tokens, up_sum / tokens, down_sum / tokens)
+    )
     d_pair = grad_field.reshape(pair_rows, pair_cols, channels).astype(jnp.bfloat16)
-    return (d_tokens, d_pair, total_gate / tokens, total_up / tokens, total_down / tokens)
+    return (d_tokens, d_pair, total_gate, total_up, total_down)
 
 
 def solution(mesh):
-    torus = Mesh(mesh.devices.reshape(mesh.shape["samp"], 2, 8), ("samp", "head_0", "head_1"))
+    torus = Mesh(mesh.devices.reshape(2, 4, 2, 2, 8), ("yh", "x", "core", "yl", "z"))
     return jax.shard_map(
         per_device,
         mesh=torus,
         in_specs=(
-            P("samp", None, None),
-            P("samp", None, None),
+            P(SAMP, None, None),
+            P(SAMP, None, None),
             P(None, HEAD),
             P(None, HEAD),
             P(None, HEAD),
             P(HEAD, None),
             P(HEAD, None, None),
             P(),
-            P(HEAD, "samp", None),
+            P(HEAD, SAMP, None),
             P(),
             P(),
             P(),
             P(),
         ),
-        out_specs=(P("samp", None, HEAD), P(HEAD, "samp", None), P(), P(), P()),
+        out_specs=(P(SAMP, None, HEAD), P(HEAD, SAMP, None), P(), P(), P()),
         check_vma=False,
     )

time: 340 us -> 131 us (0.39)
  waiting for transfers between devices: 262 us -> 20.7 us
  blocking collectives: 0 us -> 35.9 us
    psum x1 -> x0, waiting for transfers between devices: 252 us -> none  [in_one(): total = lax.psum(ravelled, axis)]
    all_to_all x0 -> x3, blocking collectives: none -> 35.9 us  [exchange(): return lax.all_to_all(pieces, axes, 0, 0, tiled=True)]
    reduce_scatter x2, waiting for transfers between devices: 0.02 us -> 8.8 us  [sum_in_order(): pieces = lax.psum_scatter(pieces, axes[k], scatter_dimension=0, tiled=True)]
  transfers between devices with their start and end apart: 5 -> 6, of which waited for: 3 -> 5; matrix products, arithmetic and copies ran while one was open for 8% -> 18% of each run, Pallas kernels for 0% -> 0%
where the time goes in v1:
time: 131 us; the launch traced here: 130 us
  blocking collectives  35.9 us (27%)
  matrix products  21.6 us (16%)
  waiting for transfers between devices  20.7 us (16%)
  starting transfers between devices  16.8 us (13%)
  between operations  15.5 us (12%)
  other arithmetic  9.97 us (8%)
  local copies, waits for them, and re-layouts  9.52 us (7%)
    all_to_all x3, blocking collectives, exchange(): return lax.all_to_all(pieces, axes, 0, 0, tiled=True)  35.9 us
    all_to_all x1, starting transfers between devices, per_device(): lax.all_to_all(summed.astype(jnp.bfloat16), HEAD, split_axis=1, concat_ax...  8.84 us
    reduce_scatter x2, waiting for transfers between devices, sum_in_order(): pieces = lax.psum_scatter(pieces, axes[k], scatter_dimension=0, tiled=True)  8.8 us
    all_to_all x1, starting transfers between devices, sent_and_summed(): lax.all_to_all(cut_along(array, dim, length), axis, 0, 0, tiled=True)  7.62 us
    all_to_all x1, waiting for transfers between devices, per_device(): lax.all_to_all(summed.astype(jnp.bfloat16), HEAD, split_axis=1, concat_ax...  5.28 us
    all_to_all x1, waiting for transfers between devices, sent_and_summed(): lax.all_to_all(cut_along(array, dim, length), axis, 0, 0, tiled=True)  3.75 us
    dot_general x2, matrix products, layer_forward(): up_proj = jnp.dot(normed_low, up_weight, preferred_element_type=jnp.float32)  3.41 us
    dot_general x2, matrix products, layer_backward(): jnp.dot(grad_low, down_weight.T, preferred_element_type=jnp.float32)  2.89 us
  transfers between devices with their start and end apart: 6, of which 5 were waited for; matrix products, arithmetic and copies ran while one was open for 18% of the time, Pallas kernels for 0%

profile of v1, /device:TPU:2, one launch (start us, length us, event | category | flops | bytes accessed | tf_op | source)
XLA Modules:
  0.0 130.1 jit_solution(14637688876788549491)
XLA Ops:
  7.3 1.3 bitcast_convert_fusion
  8.6 1.3 %copy.59 = f32[512,512]{0,1:T(8,128)} copy(f32[512,512]{1,0:T(8,128)S(1)} %bitcast_convert_fusion) | data formatting | bytes 2097152 | tf_op jit(solution)/shard_map/while/body/eval_jaxpr/add | solution.py:165
  10.7 0.7 convolution_convert_fusion.1
  11.4 0.6 convolution_convert_fusion.3
  12.1 2.3 %fusion.71 = (f32[2,512]{1,0:T(2,128)S(1)}, f32[2,512,512]{1,2,0:T(8,128)}) fusion(f32[512,512]{0,1:T(8,128)S(1)} %copy-done.8, pred[512]{0:T(512)(128)(4,1)S(1)} %iota_compare_fusion, bf16[3,1,2,512,48]{3,4,2,1,0:T(8,128)(2,1)S(1)} %bitcast.181), kind=kOutput, calls=%fused_computation.136 | convolution fusion | flops 52953600 | bytes 3346944 | tf_op jit(solution)/shard_map/while/body/eval_jaxpr/sub | solution.py:171
  14.3 1.1 convolution_convert_fusion.2
  15.5 2.2 %multiply_reduce_fusion = (f32[2,512]{1,0:T(2,128)S(1)}, f32[2,512,512]{1,2,0:T(8,128)S(1)}) fusion(f32[2,512,512]{1,2,0:T(8,128)} %get-tuple-element.59, f32[2,512]{1,0:T(2,128)S(1)} %get-tuple-element.58, bf16[2,512,48]{1,2,0:T(8,128)(2,1)S(1)} %convolution_convert_fusion.3, bf16[3,1,2,512,48]{3,4,2,1,0:T(8,128)(2,1)S(1)} %bitcast.183), kind=kOutput, calls=%fused_computation.2 | convolution fusion | flops 51903488 | bytes 4399104 | tf_op jit(solution)/shard_map/while/body/eval_jaxpr/sie,sje->sij/dot_general | solution.py:174
  17.7 1.5 %fusion.9 = (bf16[512,512]{0,1:T(8,128)(2,1)}, bf16[2,512,512]{1,2,0:T(8,128)(2,1)S(1)}) fusion(f32[2,512,512]{1,2,0:T(8,128)S(1)} %get-tuple-element.61, f32[2,512]{1,0:T(2,128)S(1)} %get-tuple-element.60, f32[2,512,512]{1,2,0:T(8,128)S(1)} %copy-done.2, f32[2,512]{1,0:T(2,128)S(1)} %get-tuple-element.58), kind=kLoop, calls=%fused_computation.37 | loop fusion | flops 2359296 | bytes 5775360 | tf_op jit(solution)/shard_map/while/body/eval_jaxpr/reduce_sum | solution.py:181
  19.2 0.4 fusion.2
  19.6 0.3 fusion.3
  19.9 1.8 %convolution_convert_fusion = bf16[2,512,768]{2,1,0:T(8,128)(2,1)} fusion(bf16[2,512,48]{1,2,0:T(8,128)(2,1)S(1)} %convolution_convert_fusion.2, bf16[2,512,48]{1,2,0:T(8,128)(2,1)S(1)} %fusion.2, bf16[2,512,48]{1,2,0:T(8,128)(2,1)S(1)} %fusion.3, bf16[768,48]{0,1:T(8,128)(2,1)S(1)} %copy-done.22, bf16[768,48]{0,1:T(8,128)(2,1)S(1)} %copy-done.23, ...), kind=kOutput, calls=%fused_computation.6 | convolution fusion | flops 228827136 | bytes 2088960 | tf_op jit(solution)/shard_map/tla,ua->tlu/dot_general | solution.py:205
  21.7 1.7 %copy.63 = bf16[2,512,768]{1,2,0:T(8,128)(2,1)S(1)} copy(bf16[2,512,768]{2,1,0:T(8,128)(2,1)} %convolution_convert_fusion) | data formatting | bytes 3145728 | tf_op jit(solution)/shard_map/convert_element_type | solution.py:207
  23.4 1.3 copy.64
  24.8 7.6 %all-to-all-start = ((bf16[16,1,512,32]{2,3,1,0:T(8,128)(2,1)}), bf16[16,1,512,32]{2,3,1,0:T(8,128)(2,1)}, u32[]{:S(2)}, u32[]{:S(2)}) async-start(bf16[16,1,512,32]{2,3,1,0:T(8,128)(2,1)} %bitcast.176), calls=%async_computation.2 | async-start | bytes 1048576 | tf_op jit(solution)/shard_map/all_to_all | solution.py:41
  32.6 0.4 multiply_reduce_fusion.4
  33.0 0.3 multiply_convert_fusion.6
  33.7 1.3 multiply_convert_fusion.5
  35.0 0.4 fusion.72
  35.4 0.4 multiply_reduce_fusion.3
  35.8 0.3 fusion.13
  36.1 1.2 fusion.36
  37.4 3.8 %all-to-all-done = bf16[16,1,512,32]{2,3,1,0:T(8,128)(2,1)} async-done(((bf16[16,1,512,32]{2,3,1,0:T(8,128)(2,1)}), bf16[16,1,512,32]{2,3,1,0:T(8,128)(2,1)}, u32[]{:S(2)}, u32[]{:S(2)}) %all-to-all-start) | async-done | bytes 524320 | tf_op jit(solution)/shard_map/all_to_all | solution.py:41
  41.1 1.1 bitcast_reduce_fusion
  42.4 0.5 broadcast.165
  43.0 1.4 %reduce.6 = bf16[512,32]{1,0:T(8,128)(2,1)S(1)} reduce(bf16[512,1,32]{2,1,0:T(2,128)(2,1)S(1)} %bitcast.177, bf16[]{:T(256)} %broadcast.165), dimensions={1}, to_apply=%bitcast.125.reduce_sub_computation | reduce | bytes 65538
  44.4 0.8 reshape.195
  45.2 8.8 %all-to-all-start.1 = ((bf16[16,2,512]{2,1,0:T(2,128)(2,1)}), bf16[16,2,512]{2,1,0:T(2,128)(2,1)S(1)}, u32[]{:S(2)}, u32[]{:S(2)}) async-start(bf16[16,2,512]{2,1,0:T(2,128)(2,1)} %reshape.195), calls=%async_computation.3 | async-start | bytes 65536 | tf_op jit(solution)/shard_map/all_to_all | solution.py:211
  54.2 2.1 %fusion.39 = f32[1024,256]{1,0:T(8,128)} fusion(bf16[1024,128]{1,0:T(8,128)(2,1)S(1)} %fusion.13, bf16[2,128,256]{2,1,0:T(8,128)(2,1)} %param.24), kind=kOutput, calls=%fused_computation.95 | convolution fusion | flops 67108864 | bytes 1376256 | tf_op jit(solution)/shard_map/dot_general | solution.py:84
  56.5 0.8 rsqrt.22
  57.2 5.3 %all-to-all-done.1 = bf16[16,2,512]{2,1,0:T(2,128)(2,1)S(1)} async-done(((bf16[16,2,512]{2,1,0:T(2,128)(2,1)}), bf16[16,2,512]{2,1,0:T(2,128)(2,1)S(1)}, u32[]{:S(2)}, u32[]{:S(2)}) %all-to-all-start.1) | async-done | bytes 32800 | tf_op jit(solution)/shard_map/all_to_all | solution.py:211
  63.6 2.3 %multiply_convert_fusion.3 = (bf16[1024,256]{1,0:T(8,128)(2,1)S(1)}, bf16[1024,256]{1,0:T(8,128)(2,1)S(1)}) fusion(f32[1024,256]{1,0:T(8,128)} %fusion.36, f32[1024,256]{1,0:T(8,128)} %fusion.39, bf16[2,256,128]{2,1,0:T(8,128)(2,1)} %param.25, f32[1024,128]{1,0:T(8,128)S(1)} %fusion.73), kind=kOutput, calls=%fused_computation.26 | convolution fusion | flops 70647808 | bytes 3735552 | tf_op jit(solution)/shard_map/dot_general | solution.py:95
  65.9 0.5 convolution_bitcast_fusion.2
  66.5 0.4 copy-done.10
  67.7 0.7 fusion.69
  68.4 0.6 multiply_add_fusion
  69.3 0.6 multiply_convert_fusion.1
  69.9 0.3 fusion.47
  70.2 0.7 fusion.68
  70.9 1.3 %fusion.12 = (bf16[1024,128]{1,0:T(8,128)(2,1)S(1)}, bf16[1024,128]{1,0:T(8,128)(2,1)}) fusion(bf16[32,32,128]{2,1,0:T(8,128)(2,1)S(1)} %copy-done.1, f32[1024]{0:T(1024)S(1)} %div.65, f32[1024]{0:T(1024)S(1)} %rsqrt.22, f32[1024,128]{1,0:T(8,128)S(1)} %multiply_add_fusion, f32[1024]{0:T(1024)S(1)} %broadcast_multiply_fusion.1, ...), kind=kLoop, calls=%fused_computation.52 | loop fusion | flops 1310720 | bytes 1851392 | tf_op jit(solution)/shard_map/convert_element_type | solution.py:82
  73.0 0.3 convolution_bitcast_fusion.3
  73.6 1.4 %collective-permute-done = bf16[16,48,128]{2,1,0:T(8,128)(2,1)S(1)} collective-permute-done((bf16[16,48,128]{2,1,0:T(8,128)(2,1)S(1)}, bf16[16,48,128]{2,1,0:T(8,128)(2,1)S(1)}, u32[]{:S(2)}, u32[]{:S(2)}) %collective-permute-start) | collective-permute-done | bytes 196640 | tf_op jit(solution)/shard_map/ppermute | solution.py:54
  75.1 13.2 %all_to_all.32 = bf16[16,48,128]{2,1,0:T(8,128)(2,1)S(1)} all-to-all(bf16[16,48,128]{2,1,0:T(8,128)(2,1)S(1)} %fusion.14), channel_id=1, replica_groups=mesh['yh'=2,'x'=4,'core'=2,'yl'=2,'z'=8] {'yh','x','yl'}, dimensions={0} | all-to-all | bytes 393216 | tf_op jit(solution)/shard_map/all_to_all | solution.py:46
  88.3 11.1 %all_to_all.33 = bf16[8,48,128]{2,1,0:T(8,128)(2,1)S(1)} all-to-all(bf16[8,48,128]{2,1,0:T(8,128)(2,1)S(1)} %broadcast_in_dim.53), channel_id=1, replica_groups=mesh['yh'=2,'x'=4,'core'=2,'yl'=2,'z'=8] {'z'}, dimensions={0} | all-to-all | bytes 196608 | tf_op jit(solution)/shard_map/all_to_all | solution.py:46
  99.5 11.6 %all_to_all.34 = bf16[16,48,128]{2,1,0:T(8,128)(2,1)S(1)} all-to-all(bf16[16,48,128]{2,1,0:T(8,128)(2,1)S(1)} %broadcast_in_dim.54), channel_id=1, replica_groups=mesh['yh'=2,'x'=4,'core'=2,'yl'=2,'z'=8] {'yh','x','yl'}, dimensions={0} | all-to-all | bytes 393216 | tf_op jit(solution)/shard_map/all_to_all | solution.py:46
  111.1 1.4 %collective-permute-done.1 = bf16[16,48,128]{2,1,0:T(8,128)(2,1)S(1)} collective-permute-done((bf16[16,48,128]{2,1,0:T(8,128)(2,1)S(1)}, bf16[16,48,128]{2,1,0:T(8,128)(2,1)S(1)}, u32[]{:S(2)}, u32[]{:S(2)}) %collective-permute-start.1) | collective-permute-done | bytes 196640 | tf_op jit(solution)/shard_map/ppermute | solution.py:54
  112.9 0.7 slice_convert_fusion
  113.6 0.8 fusion.70
  114.5 8.8 %reduce-scatter.5.cloned.1.call-done = bf16[1,2,512,48]{2,3,1,0:T(8,128)(2,1)} async-done(((bf16[2,2,512,48]{2,3,1,0:T(8,128)(2,1)}), bf16[1,2,512,48]{2,3,1,0:T(8,128)(2,1)}) %reduce-scatter.5.cloned.1.call-update) | async-done | bytes 98320 | tf_op jit(solution)/shard_map/reduce_scatter | solution.py:24
  (96 shorter events, 4.8 us)
Async XLA Ops:
  7.2 3.5 %copy-start = (bf16[2,512,768]{2,1,0:T(8,128)(2,1)S(1)}, bf16[2,512,768]{2,1,0:T(8,128)(2,1)}, u32[]{:S(2)}) copy-start(bf16[2,512,768]{2,1,0:T(8,128)(2,1)} %param.13) | copy-start | bytes 4718596
  7.2 3.5 %copy-start.22 = (bf16[768,48]{0,1:T(8,128)(2,1)S(1)}, bf16[768,48]{0,1:T(8,128)(2,1)}, u32[]{:S(2)}) copy-start(bf16[768,48]{0,1:T(8,128)(2,1)} %param.17) | copy-start | bytes 221188
  7.2 3.5 %copy-start.23 = (bf16[768,48]{0,1:T(8,128)(2,1)S(1)}, bf16[768,48]{0,1:T(8,128)(2,1)}, u32[]{:S(2)}) copy-start(bf16[768,48]{0,1:T(8,128)(2,1)} %param.16) | copy-start | bytes 221188
  7.2 3.5 %copy-start.24 = (bf16[768,48]{0,1:T(8,128)(2,1)S(1)}, bf16[768,48]{0,1:T(8,128)(2,1)}, u32[]{:S(2)}) copy-start(bf16[768,48]{0,1:T(8,128)(2,1)} %param.15) | copy-start | bytes 221188
  7.2 105.7 %reduce-scatter.3.cloned.1.call-start = ((), (), s32[]{:S(2)}) async-start(), calls=%async_computation.7 | async-start | bytes 1769472 | tf_op jit(solution)/shard_map/reduce_scatter | solution.py:24
  8.5 2.9 %copy-start.16 = (bf16[48,768]{1,0:T(8,128)(2,1)S(1)}, bf16[48,768]{1,0:T(8,128)(2,1)}, u32[]{:S(2)}) copy-start(bf16[48,768]{1,0:T(8,128)(2,1)} %param.18) | copy-start | bytes 221188
  9.9 1.5 %copy-start.3 = (bf16[2,512,768]{2,1,0:T(8,128)(2,1)S(1)}, bf16[2,512,768]{2,1,0:T(8,128)(2,1)}, u32[]{:S(2)}) copy-start(bf16[2,512,768]{2,1,0:T(8,128)(2,1)} %param.14) | copy-start | bytes 4718596
  10.7 1.3 %copy-start.8 = (f32[512,512]{0,1:T(8,128)S(1)}, f32[512,512]{0,1:T(8,128)}, u32[]{:S(2)}) copy-start(f32[512,512]{0,1:T(8,128)} %copy.59) | copy-start | bytes 3145732
  15.5 2.3 %copy-start.2 = (f32[2,512,512]{1,2,0:T(8,128)S(1)}, f32[2,512,512]{1,2,0:T(8,128)}, u32[]{:S(2)}) copy-start(f32[2,512,512]{1,2,0:T(8,128)} %get-tuple-element.59) | copy-start | bytes 6291460
  24.7 7.7 %copy-start.1 = (bf16[32,32,128]{2,1,0:T(8,128)(2,1)S(1)}, bf16[32,32,128]{2,1,0:T(8,128)(2,1)}, u32[]{:S(2)}) copy-start(bf16[32,32,128]{2,1,0:T(8,128)(2,1)} %param.21) | copy-start | bytes 786436
  24.7 8.6 %copy-start.9 = (bf16[2,128,256]{2,1,0:T(8,128)(2,1)S(1)}, bf16[2,128,256]{2,1,0:T(8,128)(2,1)}, u32[]{:S(2)}) copy-start(bf16[2,128,256]{2,1,0:T(8,128)(2,1)} %param.23) | copy-start | bytes 393220
  24.8 8.9 %copy-start.11 = (bf16[2,128,256]{2,1,0:T(8,128)(2,1)S(1)}, bf16[2,128,256]{2,1,0:T(8,128)(2,1)}, u32[]{:S(2)}) copy-start(bf16[2,128,256]{2,1,0:T(8,128)(2,1)} %param.24) | copy-start | bytes 393220
  24.8 16.4 %all-to-all-start = ((bf16[16,1,512,32]{2,3,1,0:T(8,128)(2,1)}), bf16[16,1,512,32]{2,3,1,0:T(8,128)(2,1)}, u32[]{:S(2)}, u32[]{:S(2)}) async-start(bf16[16,1,512,32]{2,3,1,0:T(8,128)(2,1)} %bitcast.176), calls=%async_computation.2 | async-start | bytes 1048576 | tf_op jit(solution)/shard_map/all_to_all | solution.py:41
  33.0 2.0 %copy-start.13 = (f32[32,32]{1,0:T(8,128)}, f32[32,32]{1,0:T(8,128)S(1)}, u32[]{:S(2)}) copy-start(f32[32,32]{1,0:T(8,128)S(1)} %add_rsqrt_fusion) | copy-start | bytes 12292
  33.7 1.3 %copy-start.4 = (f32[1024,256]{1,0:T(8,128)}, f32[1024,256]{1,0:T(8,128)S(1)}, u32[]{:S(2)}) copy-start(f32[1024,256]{1,0:T(8,128)S(1)} %fusion.49) | copy-start | bytes 3145732
  33.7 1.3 copy-start.19
  35.4 6.9 %copy-start.14 = (f32[1024]{0:T(1024)}, f32[1024]{0:T(1024)S(1)}, u32[]{:S(2)}) copy-start(f32[1024]{0:T(1024)S(1)} %broadcast_multiply_fusion.5) | copy-start | bytes 12292
  35.8 6.5 %copy-start.17 = (f32[1024]{0:T(1024)}, f32[1024]{0:T(1024)S(1)}, u32[]{:S(2)}) copy-start(f32[1024]{0:T(1024)S(1)} %add_rsqrt_fusion.1) | copy-start | bytes 12292
  45.2 18.1 %copy-start.21 = (bf16[128,16]{0,1:T(8,128)(2,1)S(1)}, bf16[128,16]{0,1:T(8,128)(2,1)}, u32[]{:S(2)}) copy-start(bf16[128,16]{0,1:T(8,128)(2,1)} %param.22) | copy-start | bytes 12292
  45.2 17.3 %all-to-all-start.1 = ((bf16[16,2,512]{2,1,0:T(2,128)(2,1)}), bf16[16,2,512]{2,1,0:T(2,128)(2,1)S(1)}, u32[]{:S(2)}, u32[]{:S(2)}) async-start(bf16[16,2,512]{2,1,0:T(2,128)(2,1)} %reshape.195), calls=%async_computation.3 | async-start | bytes 65536 | tf_op jit(solution)/shard_map/all_to_all | solution.py:211
  54.0 69.2 %reduce-scatter.5.cloned.1.call-start = ((), (), s32[]{:S(2)}) async-start(), calls=%async_computation.8 | async-start | bytes 294912 | tf_op jit(solution)/shard_map/reduce_scatter | solution.py:24
  63.6 2.3 %copy-start.6 = (f32[1024,256]{1,0:T(8,128)S(1)}, f32[1024,256]{1,0:T(8,128)}, u32[]{:S(2)}) copy-start(f32[1024,256]{1,0:T(8,128)} %fusion.36) | copy-start | bytes 3145732
  63.6 2.3 %copy-start.7 = (f32[1024,256]{1,0:T(8,128)S(1)}, f32[1024,256]{1,0:T(8,128)}, u32[]{:S(2)}) copy-start(f32[1024,256]{1,0:T(8,128)} %fusion.39) | copy-start | bytes 3145732
  65.9 0.9 copy-start.10
  66.4 1.3 copy-start.12
  66.4 1.3 copy-start.15
  66.4 1.3 copy-start.18
  67.7 1.3 %copy-start.5 = (f32[1024,256]{1,0:T(8,128)S(1)}, f32[1024,256]{1,0:T(8,128)}, u32[]{:S(2)}) copy-start(f32[1024,256]{1,0:T(8,128)} %copy-done.4) | copy-start | bytes 3145732
  67.7 1.3 %copy-start.20 = (bf16[2,256,128]{2,1,0:T(8,128)(2,1)S(1)}, bf16[2,256,128]{2,1,0:T(8,128)(2,1)}, u32[]{:S(2)}) copy-start(bf16[2,256,128]{2,1,0:T(8,128)(2,1)} %param.25) | copy-start | bytes 393220
  67.7 1.6 %copy-start.25 = (f32[1024,256]{1,0:T(8,128)S(1)}, f32[1024,256]{1,0:T(8,128)}, u32[]{:S(2)}) copy-start(f32[1024,256]{1,0:T(8,128)} %get-tuple-element.63) | copy-start | bytes 3145732
  73.5 1.5 %collective-permute-start = (bf16[16,48,128]{2,1,0:T(8,128)(2,1)S(1)}, bf16[16,48,128]{2,1,0:T(8,128)(2,1)S(1)}, u32[]{:S(2)}, u32[]{:S(2)}) collective-permute-start(bf16[16,48,128]{2,1,0:T(8,128)(2,1)S(1)} %bitcast.196), channel_id=1, source_target_pairs={{0,16},{16,0},{1,17},{17,1},{2,18},{18,2},{3,19},{19,3},{4,20},{20... | collective-permute-start | bytes 589832 | tf_op jit(solution)/shard_map/ppermute | solution.py:54
  111.1 1.4 %collective-permute-start.1 = (bf16[16,48,128]{2,1,0:T(8,128)(2,1)S(1)}, bf16[16,48,128]{2,1,0:T(8,128)(2,1)S(1)}, u32[]{:S(2)}, u32[]{:S(2)}) collective-permute-start(bf16[16,48,128]{2,1,0:T(8,128)(2,1)S(1)} %all_to_all.34), channel_id=1, source_target_pairs={{0,16},{16,0},{1,17},{17,1},{2,18},{18,2},{3,19},{19,3},{4,20},{20... | collective-permute-start | bytes 589832 | tf_op jit(solution)/shard_map/ppermute | solution.py:54
Sparse Core Ops, SparseCore 0:
  24.9 44.0 reduce-scatter.2
  113.0 10.1 reduce-scatter.4

commit v2 on v0

v2 whole, which is shorter than its diff:
```python
import math

import jax
import jax.numpy as jnp
from jax import lax
from jax.experimental import pallas as pl
from jax.experimental.pallas import tpu as pltpu
from jax.sharding import Mesh
from jax.sharding import PartitionSpec as P


HD = 48
SAMP = ("yh", "x", "core")
HEAD = ("yl", "z")
PLANE = ("yh", "x", "yl")
LANES = 128


EPS_NORM = 1e-05
MASKED = -1e30
LOW = jnp.bfloat16
WIDE = jnp.float32
VMEM = pl.BlockSpec(memory_space=pltpu.VMEM)
SMEM = pl.BlockSpec(memory_space=pltpu.SMEM)


def room(mib):
    return pltpu.CompilerParams(vmem_limit_bytes=mib << 20)


def nn(a, b):
    return lax.dot_general(a, b, (((1,), (0,)), ((), ())), preferred_element_type=WIDE)


def nt(a, b):
    return lax.dot_general(a, b, (((1,), (1,)), ((), ())), preferred_element_type=WIDE)


def tn(a, b):
    return lax.dot_general(a, b, (((0,), (0,)), ((), ())), preferred_element_type=WIDE)


def like(shape, dtype):
    return jax.ShapeDtypeStruct(shape, dtype)


def attend_kernel(
    valid, tokens, cotangent, wq, wk, wv, wo, bias, part, dscores, probs, queries, keys, grads
):
    samples, length, _ = tokens.shape
    scale = 1.0 / math.sqrt(HD)
    key_rows, value_rows = [], []
    for s in range(samples):
        x = tokens[s]
        queries[s] = nt(wq[...], x).astype(LOW)
        keys[s] = nt(wk[...], x).astype(LOW)
        grads[s] = nt(wo[...], cotangent[s]).astype(LOW)
        key_rows.append(nt(x, wk[...]).astype(LOW))
        value_rows.append(nt(x, wv[...]).astype(LOW))
    kept = lax.broadcasted_iota(jnp.int32, (length, LANES), 0) < valid[0]
    for at in range(0, length, LANES):
        block = slice(at, at + LANES)
        turned = jnp.where(kept, bias[block, :].astype(WIDE).T, MASKED)
        total = None
        for s in range(samples):
            scores = nn(key_rows[s], queries[s, :, block]) * scale + turned
            exps = jnp.exp(scores - jnp.max(scores, axis=0, keepdims=True))
            prob = exps * (1.0 / jnp.sum(exps, axis=0, keepdims=True))
            probs[s, :, block] = prob.astype(LOW)
            grad_prob = nn(value_rows[s], grads[s, :, block])
            mean = jnp.sum(prob * grad_prob, axis=0, keepdims=True)
            dscore = prob * (grad_prob - mean)
            dscores[s, :, block] = dscore.astype(LOW)
            total = dscore if total is None else total + dscore
        part[:, block] = total.astype(LOW)


def attend(valid, tokens, cotangent, wq, wk, wv, wo, bias):
    samples, length, _ = tokens.shape
    square = like((samples, length, length), LOW)
    heads = like((samples, HD, length), LOW)
    return pl.pallas_call(
        attend_kernel,
        out_shape=(like((length, length), LOW), square, square, heads, heads, heads),
        in_specs=[SMEM] + [VMEM] * 7,
        out_specs=[VMEM] * 6,
        compiler_params=room(16),
        name="attend",
    )(valid, tokens, cotangent, wq, wk, wv, wo, bias)


def token_kernel(place, dscores, probs, queries, keys, grads, wq, wk, wv, kept, sent):
    scale = 1.0 / math.sqrt(HD)
    weight = jnp.concatenate([wq[...], wk[...], wv[...]], axis=0)
    for s in range(dscores.shape[0]):
        d = dscores[s]
        joined = jnp.concatenate(
            [
                (nn(keys[s], d) * scale).astype(LOW),
                (nt(queries[s], d) * scale).astype(LOW),
                nt(grads[s], probs[s]).astype(LOW),
            ],
            axis=0,
        )
        terms = tn(weight, joined).astype(LOW)
        for r in range(16):
            z = r % 8
            slot = (z % 2 * 4 + z // 2 % 2 * 2 + z // 4) ^ place[1]
            piece = terms[r * HD : (r + 1) * HD]

            @pl.when(place[0] == r // 8)
            def _(slot=slot, piece=piece):
                kept[slot, s] = piece

            @pl.when(place[0] != r // 8)
            def _(slot=slot, piece=piece):
                sent[slot, s] = piece


def token_pieces(place, dscores, probs, queries, keys, grads, wq, wk, wv):
    samples, length, _ = dscores.shape
    half = like((8, samples, HD, length), LOW)
    return pl.pallas_call(
        token_kernel,
        out_shape=(half, half),
        in_specs=[SMEM] + [VMEM] * 8,
        out_specs=[VMEM] * 2,
        compiler_params=room(16),
        name="token_pieces",
    )(place, dscores, probs, queries, keys, grads, wq, wk, wv)


def rows_kernel(pieces, out):
    total = pieces[0].astype(WIDE)
    for k in range(1, pieces.shape[0]):
        total = total + pieces[k].astype(WIDE)
    turned = total.T.reshape(out.shape[0], LANES // total.shape[0], -1, total.shape[0])
    packed = jnp.concatenate([turned[:, q] for q in range(turned.shape[1])], axis=-1)
    out[...] = packed.astype(LOW)


def bias_rows(pieces):
    count, cols, length = pieces.shape
    return pl.pallas_call(
        rows_kernel,
        out_shape=like((count, length // count * cols // LANES, LANES), LOW),
        in_specs=[VMEM],
        out_specs=VMEM,
        compiler_params=room(4),
        name="bias_rows_sum",
    )(pieces)


def forward_kernel(pair, t_gate, t_up, t_down, normed, inv, turned, hidden_t, by_gate, by_up):
    field = pair[...].astype(WIDE)
    for layer in range(t_gate.shape[0]):
        centred = field - jnp.mean(field, axis=-1, keepdims=True)
        variance = jnp.mean(centred * centred, axis=-1, keepdims=True)
        inv_std = lax.rsqrt(variance + EPS_NORM)
        unit = centred * inv_std
        low = unit.astype(LOW)
        gate = nn(low, t_gate[layer])
        up = nn(low, t_up[layer])
        sig = jax.nn.sigmoid(gate)
        act = gate * sig
        hidden = (act * up).astype(LOW)
        normed[layer] = unit
        inv[layer] = jnp.broadcast_to(inv_std, unit.shape)
        turned[layer] = low.T
        hidden_t[layer] = hidden.T
        by_gate[layer] = up * (sig * (1.0 + gate * (1.0 - sig)))
        by_up[layer] = act
        if layer + 1 < t_gate.shape[0]:
            field = field + nn(hidden, t_down[layer])


def forward(pair, t_gate, t_up, t_down):
    pairs, channels = pair.shape
    layers, _, width = t_gate.shape
    return pl.pallas_call(
        forward_kernel,
        out_shape=(
            like((layers, pairs, channels), WIDE),
            like((layers, pairs, channels), WIDE),
            like((layers, channels, pairs), LOW),
            like((layers, width, pairs), LOW),
            like((layers, pairs, width), WIDE),
            like((layers, pairs, width), WIDE),
        ),
        in_specs=[VMEM] * 4,
        out_specs=[VMEM] * 6,
        compiler_params=room(20),
        name="pair_forward",
    )(pair, t_gate, t_up, t_down)


def backward_kernel(
    core, packed, spread, normed, inv, turned, hidden_t, by_gate, by_up, t_gate, t_up, t_down,
    d_pair, kept, sent, wide_rows, grad_top,
):
    heads = packed.shape[0]
    channels = normed.shape[2]
    rows = cols = math.isqrt(normed.shape[1])
    group = packed.shape[1]
    for q in range(LANES // cols):
        piece = packed[:, :, q * cols : (q + 1) * cols].astype(WIDE)
        for h in range(heads):
            wide_rows[h * rows + q * group : h * rows + (q + 1) * group, 0:cols] = piece[h]
    per_dot = LANES // heads
    for block in range(rows // per_dot):
        picked = jnp.concatenate(
            [
                wide_rows[pl.ds(block * per_dot + i, heads, stride=rows), :]
                for i in range(per_dot)
            ],
            axis=0,
        )
        top = nn(picked.T[0:cols].astype(LOW), spread[...])
        for i in range(per_dot):
            first = (block * per_dot + i) * cols
            grad_top[first : first + cols, :] = top[:, i * channels : (i + 1) * channels]
    grad = grad_top[...]
    share = 1.0 / (heads * rows)
    for layer in reversed(range(normed.shape[0])):
        low = grad.astype(LOW)
        down_sum = nn(hidden_t[layer], low)
        grad_hidden = nt(low, t_down[layer])
        grad_gate = (grad_hidden * by_gate[layer]).astype(LOW)
        grad_up = (grad_hidden * by_up[layer]).astype(LOW)
        gate_sum = nn(turned[layer], grad_gate)
        up_sum = nn(turned[layer], grad_up)
        for m, weight_sum in enumerate((gate_sum, up_sum, down_sum)):
            if weight_sum.shape[1] != LANES:
                weight_sum = jnp.concatenate(
                    [weight_sum[:, :LANES], weight_sum[:, LANES:]], axis=0
                )
            weight_sum = (weight_sum * share).astype(LOW).reshape(16, 16, LANES)

            @pl.when(core[0] == layer)
            def _(m=m, weight_sum=weight_sum):
                kept[:, m] = weight_sum

            @pl.when(core[0] != layer)
            def _(m=m, weight_sum=weight_sum):
                sent[:, m] = weight_sum

        grad_normed = nt(grad_gate, t_gate[layer]) + nt(grad_up, t_up[layer])
        unit = normed[layer]
        grad = grad + inv[layer] * (
            grad_normed
            - jnp.mean(grad_normed, axis=-1, keepdims=True)
            - unit * jnp.mean(grad_normed * unit, axis=-1, keepdims=True)
        )
    d_pair[...] = grad.astype(LOW)


def backward(core, grad_rows, spread, saved, t_gate, t_up, t_down):
    pairs, channels = saved[0].shape[1:]
    heads, rows = grad_rows.shape[0], math.isqrt(pairs)
    half = like((16, 3, 16, LANES), LOW)
    return pl.pallas_call(
        backward_kernel,
        out_shape=(like((pairs, channels), LOW), half, half),
        in_specs=[SMEM] + [VMEM] * 11,
        out_specs=[VMEM] * 3,
        scratch_shapes=[
            pltpu.VMEM((heads * rows, LANES), WIDE),
            pltpu.VMEM((pairs, channels), WIDE),
        ],
        compiler_params=room(20),
        name="pair_backward",
    )(core, grad_rows, spread, *saved, t_gate, t_up, t_down)


def exchange(pieces, axes):
    return lax.all_to_all(pieces, axes, 0, 0, tiled=True)


def summed(pieces):
    return jnp.sum(pieces.astype(WIDE), axis=0).astype(LOW)


def flipped(array, axis, bit):
    return lax.ppermute(array, axis, [(k, k ^ bit) for k in range(lax.axis_size(axis))])


def added(kept, received):
    return (kept.astype(WIDE) + received.astype(WIDE)).astype(LOW)


def copies(block, count):
    return jnp.broadcast_to(block, (count, *block.shape))


def sum_everywhere(kept, sent):
    half = added(kept, flipped(sent, "core", 1))
    block = summed(exchange(half, PLANE))
    block = summed(exchange(copies(block, 8), "z"))
    half = exchange(copies(block, 16), PLANE)
    other = flipped(half, "core", 1)
    second = lax.axis_index("core") == 1
    layers = jnp.stack([jnp.where(second, other, half), jnp.where(second, half, other)])
    layers = layers.astype(WIDE).reshape(2, 16, 3, 16, LANES)
    gate, up, down = (layers[:, :, m].reshape(2, 256, LANES) for m in range(3))

    def wide(a):
        return a.reshape(2, 2, 128, LANES).transpose(0, 2, 1, 3).reshape(2, 128, 256)

    return wide(gate), wide(up), down


def token_sum(kept, sent):
    piece = added(kept, flipped(sent, "yl", 1))
    for bit in (1, 2, 4):
        count = piece.shape[0] // 2
        piece = added(piece[:count], flipped(piece[count:], "z", bit))
    return piece[0]


def per_device(
    input_tokens,
    output_cotangent,
    query_weight,
    key_weight,
    value_weight,
    output_weight,
    pair_bias,
    valid_len,
    pair_in,
    w_bias,
    t_gate,
    t_up,
    t_down,
):
    tokens = input_tokens.shape[1]
    rows, cols, channels = pair_in.shape
    heads = w_bias.shape[1]
    wq, wk, wv = query_weight.T, key_weight.T, value_weight.T
    core = lax.axis_index("core").reshape(1)
    z = lax.axis_index("z")
    place = jnp.stack([lax.axis_index("yl"), z % 2 * 4 + z // 2 % 2 * 2 + z // 4])
    part, dscores, probs, queries, keys, grads = attend(
        valid_len, input_tokens, output_cotangent, wq, wk, wv, output_weight, pair_bias[0]
    )
    received = exchange(part.reshape(16, tokens // 16, tokens), SAMP)
    kept, sent = token_pieces(place, dscores, probs, queries, keys, grads, wq, wk, wv)
    saved = forward(pair_in.reshape(rows * cols, channels), t_gate, t_up, t_down)
    per_dot = LANES // heads
    spread = jnp.einsum("ij,ch->ihjc", jnp.eye(per_dot, dtype=LOW), w_bias)
    spread = spread.reshape(LANES, per_dot * channels)
    grad_rows = exchange(bias_rows(received), HEAD)
    d_tokens = token_sum(kept, sent)
    d_pair, own, other = backward(core, grad_rows, spread, saved, t_gate, t_up, t_down)
    d_gate, d_up, d_down = sum_everywhere(own.reshape(16, 48, LANES), other.reshape(16, 48, LANES))
    return (d_tokens.transpose(0, 2, 1), d_pair.reshape(rows, cols, channels), d_gate, d_up, d_down)


def solution(mesh):
    torus = Mesh(mesh.devices.reshape(2, 4, 2, 2, 8), ("yh", "x", "core", "yl", "z"))
    return jax.shard_map(
        per_device,
        mesh=torus,
        in_specs=(
            P(SAMP, None, None),
            P(SAMP, None, None),
            P(None, HEAD),
            P(None, HEAD),
            P(None, HEAD),
            P(HEAD, None),
            P(HEAD, None, None),
            P(),
            P(HEAD, SAMP, None),
            P(),
            P(),
            P(),
            P(),
        ),
        out_specs=(P(SAMP, None, HEAD), P(HEAD, SAMP, None), P(), P(), P()),
        check_vma=False,
    )
```

time: 340 us -> 126 us (0.37)
  waiting for transfers between devices: 262 us -> 29.6 us
  matrix products: 21.6 us -> 0 us
  starting transfers between devices: 16.8 us -> 35.5 us
  Pallas kernels: 0 us -> 16.4 us
  between operations: 16.9 us -> 1.51 us
  blocking collectives: 0 us -> 14 us
  local copies, waits for them, and re-layouts: 10.7 us -> 24.5 us
  other arithmetic: 11.8 us -> 3.26 us
    psum x1 -> x0, waiting for transfers between devices: 252 us -> none  [in_one(): total = lax.psum(ravelled, axis)]
    dot_general x25 -> x0, matrix products: 19.3 us -> none  [the longest x2 3.44 us: layer_forward(): up_proj = jnp.dot(normed_low, up_weight, preferred_element_type=jnp.float32)]
    unnamed x57 -> x55, local copies, waits for them, and re-layouts: 3.14 us -> 22.2 us
    pallas_call x0 -> x5, Pallas kernels: none -> 16.4 us  [the longest x1 5.01 us: backward(): pl.pallas_call(backward_kernel, out_shape=(like((pairs, channels), LOW),...]
    all_to_all x2 -> x4, waiting for transfers between devices: 8.98 us -> 23.3 us  [exchange(): return lax.all_to_all(pieces, axes, 0, 0, tiled=True)]
    all_to_all x0 -> x1, blocking collectives: none -> 14 us  [exchange(): return lax.all_to_all(pieces, axes, 0, 0, tiled=True)]
    all_to_all x2 -> x4, starting transfers between devices: 16.5 us -> 27.1 us  [exchange(): return lax.all_to_all(pieces, axes, 0, 0, tiled=True)]
    ppermute x0 -> x6, starting transfers between devices: none -> 8.42 us  [flipped(): lax.ppermute(array, axis, [(k, k ^ bit) for k in range(lax.axis_size(axis...]
  transfers between devices with their start and end apart: 5 -> 10, of which waited for: 3 -> 5; matrix products, arithmetic and copies ran while one was open for 8% -> 3% of each run, Pallas kernels for 0% -> 6%
where the time goes in v2:
time: 126 us; the launch traced here: 125 us
  starting transfers between devices  35.5 us (28%)
  waiting for transfers between devices  29.6 us (23%)
  local copies, waits for them, and re-layouts  24.5 us (19%)
  Pallas kernels  16.4 us (13%)
  blocking collectives  14 us (11%)
  other arithmetic  3.26 us (3%)
  between operations  1.51 us (1%)
    all_to_all x4, starting transfers between devices, exchange(): return lax.all_to_all(pieces, axes, 0, 0, tiled=True)  27.1 us
    all_to_all x4, waiting for transfers between devices, exchange(): return lax.all_to_all(pieces, axes, 0, 0, tiled=True)  23.3 us
    unnamed x55, local copies, waits for them, and re-layouts  22.2 us
    all_to_all x1, blocking collectives, exchange(): return lax.all_to_all(pieces, axes, 0, 0, tiled=True)  14 us
    ppermute x6, starting transfers between devices, flipped(): lax.ppermute(array, axis, [(k, k ^ bit) for k in range(lax.axis_size(axis...  8.42 us
    ppermute x6, waiting for transfers between devices, flipped(): lax.ppermute(array, axis, [(k, k ^ bit) for k in range(lax.axis_size(axis...  6.24 us
    pallas_call x1, Pallas kernels, backward(): pl.pallas_call(backward_kernel, out_shape=(like((pairs, channels), LOW),...  5.01 us
    pallas_call x1, Pallas kernels, attend(): pl.pallas_call(attend_kernel, out_shape=(like((length, length), LOW), squ...  4.91 us
  transfers between devices with their start and end apart: 10, of which 5 were waited for; matrix products, arithmetic and copies ran while one was open for 3% of the time, Pallas kernels for 6%

profile of v2, /device:TPU:2, one launch (start us, length us, event | category | flops | bytes accessed | tf_op | source)
XLA Modules:
  0.0 124.7 jit_solution(14138232671002075744)
XLA Ops:
  1.4 1.4 %copy-done.2 = bf16[2,512,768]{2,1,0:T(8,128)(2,1)S(1)} copy-done((bf16[2,512,768]{2,1,0:T(8,128)(2,1)S(1)}, bf16[2,512,768]{2,1,0:T(8,128)(2,1)}, u32[]{:S(2)}) %copy-start.2) | copy-done | bytes 1572888
  2.8 1.4 %copy-done.3 = bf16[2,512,768]{2,1,0:T(8,128)(2,1)S(1)} copy-done((bf16[2,512,768]{2,1,0:T(8,128)(2,1)S(1)}, bf16[2,512,768]{2,1,0:T(8,128)(2,1)}, u32[]{:S(2)}) %copy-start.3) | copy-done | bytes 1572888
  4.2 1.0 copy-done.15
  5.3 0.9 copy-done.18
  6.1 0.9 copy-done.20
  7.0 0.9 copy-done.22
  7.9 0.9 copy-done.25
  8.8 4.9 %attend.1 = (bf16[512,512]{1,0:T(8,128)(2,1)}, bf16[2,512,512]{2,1,0:T(8,128)(2,1)S(1)}, bf16[2,512,512]{2,1,0:T(8,128)(2,1)S(1)}, bf16[2,48,512]{2,1,0:T(8,128)...) custom-call(s32[1]{0:T(128)S(6)} %copy.31.valid, bf16[2,512,768]{2,1,0:T(8,128)(2,1)S(1)} %copy-done.2, ...), custom_call_target="tpu_custom_call" | custom-call | tf_op jit(solution)/shard_map/attend/pallas_call | solution.py:82
  13.7 3.7 %token_pieces.1 = (bf16[8,2,48,512]{3,2,1,0:T(8,128)(2,1)S(1)}, bf16[8,2,48,512]{3,2,1,0:T(8,128)(2,1)}) custom-call(s32[2]{0:T(128)S(1)} %pad_add_fusion.place, bf16[2,512,512]{2,1,0:T(8,128)(2,1)S(1)} %get-tuple-element.22.dscores, bf16[2,512,512]{2,1,0:T(8,128)(2,1)S(1)} %get-tuple-element.23.probs, bf16[2,48,512]{2,1,0:T(8,128)(2,1)S(1)} %get-tuple-element.24.queries, ...), custom_call_target="tpu_custom_call" | custom-call | tf_op jit(solution)/shard_map/token_pieces/pallas_call | solution.py:123
  17.4 0.9 copy-done.8
  18.3 1.6 %collective-permute-start = (bf16[8,2,48,512]{3,2,1,0:T(8,128)(2,1)}, bf16[8,2,48,512]{3,2,1,0:T(8,128)(2,1)}, u32[]{:S(2)}, u32[]{:S(2)}) collective-permute-start(bf16[8,2,48,512]{3,2,1,0:T(8,128)(2,1)} %get-tuple-element.28), channel_id=1, source_target_pairs={{0,8},{8,0},{1,9},{9,1},{2,10},{10,2},{3,11},{11,3},{4,12},{12,4},... | collective-permute-start | bytes 2359304 | tf_op jit(solution)/shard_map/ppermute | solution.py:284
  19.9 7.2 %all-to-all-start = ((bf16[16,32,512]{2,1,0:T(8,128)(2,1)}), bf16[16,32,512]{2,1,0:T(8,128)(2,1)S(1)}, u32[]{:S(2)}, u32[]{:S(2)}) async-start(bf16[16,32,512]{2,1,0:T(8,128)(2,1)} %bitcast.9), calls=%async_computation | async-start | bytes 1048576 | tf_op jit(solution)/shard_map/all_to_all | solution.py:276
  27.1 18.4 %all-to-all-done.pieces = bf16[16,32,512]{2,1,0:T(8,128)(2,1)S(1)} async-done(((bf16[16,32,512]{2,1,0:T(8,128)(2,1)}), bf16[16,32,512]{2,1,0:T(8,128)(2,1)S(1)}, u32[]{:S(2)}, u32[]{:S(2)}) %all-to-all-start) | async-done | bytes 524320 | tf_op jit(solution)/shard_map/all_to_all | solution.py:276
  45.5 0.9 bias_rows_sum.1
  46.4 8.6 %all-to-all-start.1 = ((bf16[16,8,128]{2,1,0:T(8,128)(2,1)}), bf16[16,8,128]{2,1,0:T(8,128)(2,1)}, u32[]{:S(2)}, u32[]{:S(2)}) async-start(bf16[16,8,128]{2,1,0:T(8,128)(2,1)} %bias_rows_sum.1), calls=%async_computation.1 | async-start | bytes 65536 | tf_op jit(solution)/shard_map/all_to_all | solution.py:276
  55.0 0.1 broadcast_multiply_fusion
  55.2 0.9 copy-done.11
  56.1 0.9 copy-done.13
  57.0 0.9 copy-done.24
  58.0 1.9 %pair_forward.1 = (f32[2,1024,128]{2,1,0:T(8,128)S(1)}, f32[2,1024,128]{2,1,0:T(8,128)S(1)}, bf16[2,128,1024]{2,1,0:T(8,128)(2,1)S(1)}, bf16[2,256,1024]{2,1,0:T...) custom-call(bf16[1024,128]{1,0:T(8,128)(2,1)S(1)} %bitcast.47, ...), custom_call_target="tpu_custom_call" | custom-call | tf_op jit(solution)/shard_map/pair_forward/pallas_call | solution.py:180
  59.9 1.4 %copy-done = f32[2,1024,256]{2,1,0:T(8,128)} copy-done((f32[2,1024,256]{2,1,0:T(8,128)}, f32[2,1024,256]{2,1,0:T(8,128)S(1)}, u32[]{:S(2)}) %copy-start) | copy-done | bytes 2097176
  61.2 1.0 copy-done.4
  62.2 1.0 copy-done.6
  63.2 0.8 copy-done.16
  64.0 1.6 %copy-done.1 = f32[2,1024,256]{2,1,0:T(8,128)S(1)} copy-done((f32[2,1024,256]{2,1,0:T(8,128)S(1)}, f32[2,1024,256]{2,1,0:T(8,128)}, u32[]{:S(2)}) %copy-start.1) | copy-done | bytes 2097176
  65.6 1.2 copy-done.5
  66.8 1.2 copy-done.7
  68.1 0.9 copy-done.12
  69.0 0.9 copy-done.14
  69.9 1.0 copy-done.17
  70.9 5.0 %pair_backward.1 = (bf16[1024,128]{1,0:T(8,128)(2,1)}, bf16[16,3,16,128]{3,2,1,0:T(8,128)(2,1)S(1)}, bf16[16,3,16,128]{3,2,1,0:T(8,128)(2,1)S(1)}) custom-call(s32[1]{0:T(128)} %bitcast.8.core, bf16[16,8,128]{2,1,0:T(8,128)(2,1)} %all-to-all-done.1.packed, bf16[128,1024]{1,0:T(8,128)(2,1)S(1)} %bitcast.39, f32[2,1024,128]{2,1,0:T(8,128)S(1)} %get-tuple-element.30.normed, ...), custom_call_target="tpu_custom_call" | custom-call | tf_op jit(solution)/shard_map/pair_backward/pallas_call | solution.py:261
  75.9 1.4 %add_convert_fusion = bf16[8,2,48,512]{3,2,1,0:T(8,128)(2,1)S(1)} fusion(bf16[8,2,48,512]{3,2,1,0:T(8,128)(2,1)} %collective-permute-done, bf16[8,2,48,512]{3,2,1,0:T(8,128)(2,1)S(1)} %copy-done.9), kind=kLoop, calls=%fused_computation | loop fusion | flops 1572864 | bytes 2359296 | tf_op jit(solution)/shard_map/convert_element_type | solution.py:288
  77.4 1.9 %collective-permute-start.1 = (bf16[4,2,48,512]{3,2,1,0:T(8,128)(2,1)S(1)}, bf16[4,2,48,512]{3,2,1,0:T(8,128)(2,1)S(1)}, u32[]{:S(2)}, u32[]{:S(2)}) collective-permute-start(bf16[4,2,48,512]{3,2,1,0:T(8,128)(2,1)S(1)} %slice.37), channel_id=1, source_target_pairs={{0,1},{1,0},{2,3},{3,2},{4,5},{5,4},{6,7},{7,6},{8,9},{9,8},{10,11... | collective-permute-start | bytes 1179656 | tf_op jit(solution)/shard_map/ppermute | solution.py:284
  79.3 0.7 fusion
  80.1 5.7 %all-to-all-start.2 = ((bf16[16,48,128]{2,1,0:T(8,128)(2,1)}), bf16[16,48,128]{2,1,0:T(8,128)(2,1)S(1)}, u32[]{:S(2)}, u32[]{:S(2)}) async-start(bf16[16,48,128]{2,1,0:T(8,128)(2,1)} %fusion), calls=%async_computation.2 | async-start | bytes 393216 | tf_op jit(solution)/shard_map/all_to_all | solution.py:276
  85.8 3.3 %collective-permute-done.1 = bf16[4,2,48,512]{3,2,1,0:T(8,128)(2,1)S(1)} collective-permute-done((bf16[4,2,48,512]{3,2,1,0:T(8,128)(2,1)S(1)}, bf16[4,2,48,512]{3,2,1,0:T(8,128)(2,1)S(1)}, u32[]{:S(2)}, u32[]{:S(2)}) %collective-permute-start.1) | collective-permute-done | bytes 393248 | tf_op jit(solution)/shard_map/ppermute | solution.py:284
  89.1 0.1 add_convert_fusion.1
  89.2 2.7 %collective-permute-start.2 = (bf16[2,2,48,512]{3,2,1,0:T(8,128)(2,1)S(1)}, bf16[2,2,48,512]{3,2,1,0:T(8,128)(2,1)S(1)}, u32[]{:S(2)}, u32[]{:S(2)}) collective-permute-start(bf16[2,2,48,512]{3,2,1,0:T(8,128)(2,1)S(1)} %slice.39), channel_id=1, source_target_pairs={{0,2},{1,3},{2,0},{3,1},{4,6},{5,7},{6,4},{7,5},{8,10},{9,11},{10,... | collective-permute-start | bytes 589832 | tf_op jit(solution)/shard_map/ppermute | solution.py:284
  92.0 0.5 all-to-all-done.2
  92.5 14.0 %all_to_all.25 = bf16[8,48,128]{2,1,0:T(8,128)(2,1)S(1)} all-to-all(bf16[8,48,128]{2,1,0:T(8,128)(2,1)S(1)} %broadcast_in_dim.6), channel_id=1, replica_groups=mesh['yh'=2,'x'=4,'core'=2,'yl'=2,'z'=8] {'z'}, dimensions={0} | all-to-all | bytes 196608 | tf_op jit(solution)/shard_map/all_to_all | solution.py:276
  106.5 0.7 broadcast_in_dim.7
  107.2 5.5 %all-to-all-start.4 = ((bf16[16,48,128]{2,1,0:T(8,128)(2,1)}), bf16[16,48,128]{2,1,0:T(8,128)(2,1)S(1)}, u32[]{:S(2)}, u32[]{:S(2)}) async-start(bf16[16,48,128]{2,1,0:T(8,128)(2,1)} %broadcast_in_dim.7), calls=%async_computation.4 | async-start | bytes 393216 | tf_op jit(solution)/shard_map/all_to_all | solution.py:276
  112.8 2.2 %collective-permute-start.3 = (bf16[1,2,48,512]{3,2,1,0:T(8,128)(2,1)S(1)}, bf16[1,2,48,512]{3,2,1,0:T(8,128)(2,1)S(1)}, u32[]{:S(2)}, u32[]{:S(2)}) collective-permute-start(bf16[1,2,48,512]{3,2,1,0:T(8,128)(2,1)S(1)} %slice.41), channel_id=1, source_target_pairs={{0,4},{1,5},{2,6},{3,7},{4,0},{5,1},{6,2},{7,3},{8,12},{9,13},{10,... | collective-permute-start | bytes 294920 | tf_op jit(solution)/shard_map/ppermute | solution.py:284
  115.0 4.4 %all-to-all-done.4 = bf16[16,48,128]{2,1,0:T(8,128)(2,1)S(1)} async-done(((bf16[16,48,128]{2,1,0:T(8,128)(2,1)}), bf16[16,48,128]{2,1,0:T(8,128)(2,1)S(1)}, u32[]{:S(2)}, u32[]{:S(2)}) %all-to-all-start.4) | async-done | bytes 196640 | tf_op jit(solution)/shard_map/all_to_all | solution.py:276
  119.4 2.9 %collective-permute-done.3 = bf16[1,2,48,512]{3,2,1,0:T(8,128)(2,1)S(1)} collective-permute-done((bf16[1,2,48,512]{3,2,1,0:T(8,128)(2,1)S(1)}, bf16[1,2,48,512]{3,2,1,0:T(8,128)(2,1)S(1)}, u32[]{:S(2)}, u32[]{:S(2)}) %collective-permute-start.3) | collective-permute-done | bytes 98336 | tf_op jit(solution)/shard_map/ppermute | solution.py:284
  122.4 0.7 fusion.1
  123.1 0.8 fusion.3
  123.9 0.8 copy_bitcast_fusion.1
  (52 shorter events, 0.5 us)
Async XLA Ops:
  1.4 1.4 %copy-start.2 = (bf16[2,512,768]{2,1,0:T(8,128)(2,1)S(1)}, bf16[2,512,768]{2,1,0:T(8,128)(2,1)}, u32[]{:S(2)}) copy-start(bf16[2,512,768]{2,1,0:T(8,128)(2,1)} %tokens.1) | copy-start | bytes 4718596
  2.8 1.4 %copy-start.3 = (bf16[2,512,768]{2,1,0:T(8,128)(2,1)S(1)}, bf16[2,512,768]{2,1,0:T(8,128)(2,1)}, u32[]{:S(2)}) copy-start(bf16[2,512,768]{2,1,0:T(8,128)(2,1)} %cotangent.1) | copy-start | bytes 4718596
  4.2 1.0 copy-start.15
  5.3 0.9 copy-start.18
  6.1 0.9 copy-start.20
  7.0 0.9 copy-start.22
  7.9 0.9 copy-start.25
  8.8 4.9 %copy-start.19 = (bf16[768,48]{0,1:T(8,128)(2,1)S(1)}, bf16[768,48]{0,1:T(8,128)(2,1)}, u32[]{:S(2)}) copy-start(bf16[768,48]{0,1:T(8,128)(2,1)} %param.15) | copy-start | bytes 221188
  8.8 4.9 %copy-start.21 = (bf16[768,48]{0,1:T(8,128)(2,1)S(1)}, bf16[768,48]{0,1:T(8,128)(2,1)}, u32[]{:S(2)}) copy-start(bf16[768,48]{0,1:T(8,128)(2,1)} %param.16) | copy-start | bytes 221188
  8.8 4.9 %copy-start.23 = (bf16[768,48]{0,1:T(8,128)(2,1)S(1)}, bf16[768,48]{0,1:T(8,128)(2,1)}, u32[]{:S(2)}) copy-start(bf16[768,48]{0,1:T(8,128)(2,1)} %param.17) | copy-start | bytes 221188
  13.7 41.3 %copy-start.26 = (bf16[128,16]{0,1:T(8,128)(2,1)S(1)}, bf16[128,16]{0,1:T(8,128)(2,1)}, u32[]{:S(2)}) copy-start(bf16[128,16]{0,1:T(8,128)(2,1)} %param.22) | copy-start | bytes 12292
  17.4 0.9 copy-start.8
  18.3 36.9 %copy-start.10 = (bf16[2,128,256]{2,1,0:T(8,128)(2,1)S(1)}, bf16[2,128,256]{2,1,0:T(8,128)(2,1)}, u32[]{:S(2)}) copy-start(bf16[2,128,256]{2,1,0:T(8,128)(2,1)} %t_gate.3) | copy-start | bytes 393220
  18.3 57.6 %collective-permute-start = (bf16[8,2,48,512]{3,2,1,0:T(8,128)(2,1)}, bf16[8,2,48,512]{3,2,1,0:T(8,128)(2,1)}, u32[]{:S(2)}, u32[]{:S(2)}) collective-permute-start(bf16[8,2,48,512]{3,2,1,0:T(8,128)(2,1)} %get-tuple-element.28), channel_id=1, source_target_pairs={{0,8},{8,0},{1,9},{9,1},{2,10},{10,2},{3,11},{11,3},{4,12},{12,4},... | collective-permute-start | bytes 2359304 | tf_op jit(solution)/shard_map/ppermute | solution.py:284
  19.9 25.6 %all-to-all-start = ((bf16[16,32,512]{2,1,0:T(8,128)(2,1)}), bf16[16,32,512]{2,1,0:T(8,128)(2,1)S(1)}, u32[]{:S(2)}, u32[]{:S(2)}) async-start(bf16[16,32,512]{2,1,0:T(8,128)(2,1)} %bitcast.9), calls=%async_computation | async-start | bytes 1048576 | tf_op jit(solution)/shard_map/all_to_all | solution.py:276
  46.4 17.6 %all-to-all-start.1 = ((bf16[16,8,128]{2,1,0:T(8,128)(2,1)}), bf16[16,8,128]{2,1,0:T(8,128)(2,1)}, u32[]{:S(2)}, u32[]{:S(2)}) async-start(bf16[16,8,128]{2,1,0:T(8,128)(2,1)} %bias_rows_sum.1), calls=%async_computation.1 | async-start | bytes 65536 | tf_op jit(solution)/shard_map/all_to_all | solution.py:276
  55.2 0.9 copy-start.11
  56.1 0.9 copy-start.13
  57.0 0.9 copy-start.24
  59.9 1.4 %copy-start = (f32[2,1024,256]{2,1,0:T(8,128)}, f32[2,1024,256]{2,1,0:T(8,128)S(1)}, u32[]{:S(2)}) copy-start(f32[2,1024,256]{2,1,0:T(8,128)S(1)} %get-tuple-element.35.by_up) | copy-start | bytes 6291460
  61.2 1.0 copy-start.4
  62.2 1.0 copy-start.6
  63.2 0.8 copy-start.16
  64.0 1.6 %copy-start.1 = (f32[2,1024,256]{2,1,0:T(8,128)S(1)}, f32[2,1024,256]{2,1,0:T(8,128)}, u32[]{:S(2)}) copy-start(f32[2,1024,256]{2,1,0:T(8,128)} %copy-done) | copy-start | bytes 6291460
  65.6 1.2 copy-start.5
  66.8 1.2 copy-start.7
  68.1 0.9 copy-start.12
  69.0 0.9 copy-start.14
  69.9 1.0 copy-start.17
  70.9 5.0 %copy-start.9 = (bf16[8,2,48,512]{3,2,1,0:T(8,128)(2,1)S(1)}, bf16[8,2,48,512]{3,2,1,0:T(8,128)(2,1)}, u32[]{:S(2)}) copy-start(bf16[8,2,48,512]{3,2,1,0:T(8,128)(2,1)} %copy-done.8) | copy-start | bytes 2359300
  75.9 3.4 %collective-permute-start.4 = (bf16[16,48,128]{2,1,0:T(8,128)(2,1)S(1)}, bf16[16,48,128]{2,1,0:T(8,128)(2,1)S(1)}, u32[]{:S(2)}, u32[]{:S(2)}) collective-permute-start(bf16[16,48,128]{2,1,0:T(8,128)(2,1)S(1)} %bitcast.48), channel_id=1, source_target_pairs={{0,16},{16,0},{1,17},{17,1},{2,18},{18,2},{3,19},{19,3},{4,20},{20... | collective-permute-start | bytes 589832 | tf_op jit(solution)/shard_map/ppermute | solution.py:284
  77.4 11.7 %collective-permute-start.1 = (bf16[4,2,48,512]{3,2,1,0:T(8,128)(2,1)S(1)}, bf16[4,2,48,512]{3,2,1,0:T(8,128)(2,1)S(1)}, u32[]{:S(2)}, u32[]{:S(2)}) collective-permute-start(bf16[4,2,48,512]{3,2,1,0:T(8,128)(2,1)S(1)} %slice.37), channel_id=1, source_target_pairs={{0,1},{1,0},{2,3},{3,2},{4,5},{5,4},{6,7},{7,6},{8,9},{9,8},{10,11... | collective-permute-start | bytes 1179656 | tf_op jit(solution)/shard_map/ppermute | solution.py:284
  80.1 12.4 %all-to-all-start.2 = ((bf16[16,48,128]{2,1,0:T(8,128)(2,1)}), bf16[16,48,128]{2,1,0:T(8,128)(2,1)S(1)}, u32[]{:S(2)}, u32[]{:S(2)}) async-start(bf16[16,48,128]{2,1,0:T(8,128)(2,1)} %fusion), calls=%async_computation.2 | async-start | bytes 393216 | tf_op jit(solution)/shard_map/all_to_all | solution.py:276
  89.2 23.5 %collective-permute-start.2 = (bf16[2,2,48,512]{3,2,1,0:T(8,128)(2,1)S(1)}, bf16[2,2,48,512]{3,2,1,0:T(8,128)(2,1)S(1)}, u32[]{:S(2)}, u32[]{:S(2)}) collective-permute-start(bf16[2,2,48,512]{3,2,1,0:T(8,128)(2,1)S(1)} %slice.39), channel_id=1, source_target_pairs={{0,2},{1,3},{2,0},{3,1},{4,6},{5,7},{6,4},{7,5},{8,10},{9,11},{10,... | collective-permute-start | bytes 589832 | tf_op jit(solution)/shard_map/ppermute | solution.py:284
  107.2 12.2 %all-to-all-start.4 = ((bf16[16,48,128]{2,1,0:T(8,128)(2,1)}), bf16[16,48,128]{2,1,0:T(8,128)(2,1)S(1)}, u32[]{:S(2)}, u32[]{:S(2)}) async-start(bf16[16,48,128]{2,1,0:T(8,128)(2,1)} %broadcast_in_dim.7), calls=%async_computation.4 | async-start | bytes 393216 | tf_op jit(solution)/shard_map/all_to_all | solution.py:276
  112.8 9.5 %collective-permute-start.3 = (bf16[1,2,48,512]{3,2,1,0:T(8,128)(2,1)S(1)}, bf16[1,2,48,512]{3,2,1,0:T(8,128)(2,1)S(1)}, u32[]{:S(2)}, u32[]{:S(2)}) collective-permute-start(bf16[1,2,48,512]{3,2,1,0:T(8,128)(2,1)S(1)} %slice.41), channel_id=1, source_target_pairs={{0,4},{1,5},{2,6},{3,7},{4,0},{5,1},{6,2},{7,3},{8,12},{9,13},{10,... | collective-permute-start | bytes 294920 | tf_op jit(solution)/shard_map/ppermute | solution.py:284
  119.4 3.6 %collective-permute-start.5 = (bf16[16,48,128]{2,1,0:T(8,128)(2,1)S(1)}, bf16[16,48,128]{2,1,0:T(8,128)(2,1)S(1)}, u32[]{:S(2)}, u32[]{:S(2)}) collective-permute-start(bf16[16,48,128]{2,1,0:T(8,128)(2,1)S(1)} %all-to-all-done.4), channel_id=1, source_target_pairs={{0,16},{16,0},{1,17},{17,1},{2,18},{18,2},{3,19},{19,3},{4,20},{20... | collective-permute-start | bytes 589832 | tf_op jit(solution)/shard_map/ppermute | solution.py:284

commit v3 on v2

--- a/solution.py
+++ b/solution.py
@@ -22,6 +22,7 @@
 WIDE = jnp.float32
 VMEM = pl.BlockSpec(memory_space=pltpu.VMEM)
 SMEM = pl.BlockSpec(memory_space=pltpu.SMEM)
+FAR = pl.BlockSpec(memory_space=pltpu.HBM)
 
 
 def room(mib):
@@ -44,19 +45,56 @@
     return jax.ShapeDtypeStruct(shape, dtype)
 
 
+def far_away(*arrays):
+    return [pltpu.with_memory_space_constraint(a, pltpu.HBM) for a in arrays]
+
+
+def started(pairs, sems):
+    moves = [pltpu.make_async_copy(a, b, sems.at[k]) for k, (a, b) in enumerate(pairs)]
+    for move in moves:
+        move.start()
+    return moves
+
+
+def waited(moves):
+    for move in moves:
+        move.wait()
+
+
 def attend_kernel(
-    valid, tokens, cotangent, wq, wk, wv, wo, bias, part, dscores, probs, queries, keys, grads
+    valid, tokens_far, cotangent_far, wq_far, wk_far, wv_far, wo_far, bias_far,
+    part_far, dscores, probs, queries_far, keys_far, grads_far,
+    tokens, cotangent, wq, wk, wv, wo, bias, part, queries, keys, grads, sems, out_sems,
 ):
     samples, length, _ = tokens.shape
     scale = 1.0 / math.sqrt(HD)
+    moves = started(
+        [
+            (wq_far, wq),
+            (wk_far, wk),
+            (wv_far, wv),
+            (tokens_far.at[0], tokens.at[0]),
+            (wo_far, wo),
+            (cotangent_far.at[0], cotangent.at[0]),
+            (tokens_far.at[1], tokens.at[1]),
+            (cotangent_far.at[1], cotangent.at[1]),
+            (bias_far, bias),
+        ],
+        sems,
+    )
     key_rows, value_rows = [], []
     for s in range(samples):
+        waited(moves[:6] if s == 0 else moves[6:8])
         x = tokens[s]
         queries[s] = nt(wq[...], x).astype(LOW)
         keys[s] = nt(wk[...], x).astype(LOW)
         grads[s] = nt(wo[...], cotangent[s]).astype(LOW)
         key_rows.append(nt(x, wk[...]).astype(LOW))
         value_rows.append(nt(x, wv[...]).astype(LOW))
+    leaving = started(
+        [(queries, queries_far), (keys, keys_far), (grads, grads_far)], out_sems.at[0]
+    )
+    waited(moves[8:])
     kept = lax.broadcasted_iota(jnp.int32, (length, LANES), 0) < valid[0]
     for at in range(0, length, LANES):
         block = slice(at, at + LANES)
@@ -73,23 +111,34 @@
             dscores[s, :, block] = dscore.astype(LOW)
             total = dscore if total is None else total + dscore
         part[:, block] = total.astype(LOW)
+        leaving += started([(part.at[:, block], part_far.at[:, block])], out_sems.at[1, at // LANES :])
+    waited(leaving)
 
 
 def attend(valid, tokens, cotangent, wq, wk, wv, wo, bias):
     samples, length, _ = tokens.shape
     square = like((samples, length, length), LOW)
-    heads = like((samples, HD, length), LOW)
+    heads = pltpu.HBM((samples, HD, length), LOW)
     return pl.pallas_call(
         attend_kernel,
-        out_shape=(like((length, length), LOW), square, square, heads, heads, heads),
-        in_specs=[SMEM] + [VMEM] * 7,
-        out_specs=[VMEM] * 6,
+        out_shape=(pltpu.HBM((length, length), LOW), square, square, heads, heads, heads),
+        in_specs=[SMEM] + [FAR] * 7,
+        out_specs=[FAR] + [VMEM] * 2 + [FAR] * 3,
+        scratch_shapes=[
+            pltpu.VMEM(a.shape, LOW) for a in (tokens, cotangent, wq, wk, wv, wo, bias)
+        ]
+        + [pltpu.VMEM((length, length), LOW)]
+        + [pltpu.VMEM((samples, HD, length), LOW)] * 3
+        + [pltpu.SemaphoreType.DMA((9,)), pltpu.SemaphoreType.DMA((2, 4))],
         compiler_params=room(16),
         name="attend",
-    )(valid, tokens, cotangent, wq, wk, wv, wo, bias)
-
-
-def token_kernel(place, dscores, probs, queries, keys, grads, wq, wk, wv, kept, sent):
+    )(valid, *far_away(tokens, cotangent, wq, wk, wv, wo, bias))
+
+
+def token_kernel(place, dscores, probs, *refs):
+    far, (kept, sent), near, sems = refs[:6], refs[6:8], refs[8:14], refs[14]
+    queries, keys, grads, wq, wk, wv = near
+    waited(started(list(zip(far, near)), sems))
     scale = 1.0 / math.sqrt(HD)
     weight = jnp.concatenate([wq[...], wk[...], wv[...]], axis=0)
     for s in range(dscores.shape[0]):
@@ -123,11 +172,13 @@
     return pl.pallas_call(
         token_kernel,
         out_shape=(half, half),
-        in_specs=[SMEM] + [VMEM] * 8,
+        in_specs=[SMEM] + [VMEM] * 2 + [FAR] * 6,
         out_specs=[VMEM] * 2,
+        scratch_shapes=[pltpu.VMEM(a.shape, LOW) for a in (queries, keys, grads, wq, wk, wv)]
+        + [pltpu.SemaphoreType.DMA((6,))],
         compiler_params=room(16),
         name="token_pieces",
-    )(place, dscores, probs, queries, keys, grads, wq, wk, wv)
+    )(place, dscores, probs, *far_away(queries, keys, grads, wq, wk, wv))
 
 
 def rows_kernel(pieces, out):
@@ -151,9 +202,17 @@
     )(pieces)
 
 
-def forward_kernel(pair, t_gate, t_up, t_down, normed, inv, turned, hidden_t, by_gate, by_up):
+def forward_kernel(pair_far, t_gate_far, t_up_far, t_down_far, *refs):
+    far, (pair, t_gate, t_up, t_down, *near, in_sems, out_sems) = refs[:6], refs[6:]
+    normed, inv, turned, hidden_t, by_gate, by_up = near
+    layers = t_gate.shape[0]
+    moves = started(
+        [(pair_far, pair), (t_gate_far, t_gate), (t_up_far, t_up), (t_down_far, t_down)], in_sems
+    )
+    waited(moves)
     field = pair[...].astype(WIDE)
-    for layer in range(t_gate.shape[0]):
+    moves = []
+    for layer in range(layers):
         centred = field - jnp.mean(field, axis=-1, keepdims=True)
         variance = jnp.mean(centred * centred, axis=-1, keepdims=True)
         inv_std = lax.rsqrt(variance + EPS_NORM)
@@ -168,36 +227,51 @@
         inv[layer] = jnp.broadcast_to(inv_std, unit.shape)
         turned[layer] = low.T
         hidden_t[layer] = hidden.T
-        by_gate[layer] = up * (sig * (1.0 + gate * (1.0 - sig)))
-        by_up[layer] = act
-        if layer + 1 < t_gate.shape[0]:
+        by_gate[layer] = (up * (sig * (1.0 + gate * (1.0 - sig)))).astype(LOW)
+        by_up[layer] = act.astype(LOW)
+        pairs = [(a.at[layer], b.at[layer]) for a, b in zip(near, far)]
+        moves += started(pairs, out_sems.at[layer])
+        if layer + 1 < layers:
             field = field + nn(hidden, t_down[layer])
+    waited(moves)
+
+
+def saved_shapes(pairs, channels, layers, width):
+    return (
+        ((layers, pairs, channels), WIDE),
+        ((layers, pairs, channels), WIDE),
+        ((layers, channels, pairs), LOW),
+        ((layers, width, pairs), LOW),
+        ((layers, pairs, width), LOW),
+        ((layers, pairs, width), LOW),
+    )
 
 
 def forward(pair, t_gate, t_up, t_down):
-    pairs, channels = pair.shape
     layers, _, width = t_gate.shape
+    shapes = saved_shapes(*pair.shape, layers, width)
     return pl.pallas_call(
         forward_kernel,
-        out_shape=(
-            like((layers, pairs, channels), WIDE),
-            like((layers, pairs, channels), WIDE),
-            like((layers, channels, pairs), LOW),
-            like((layers, width, pairs), LOW),
-            like((layers, pairs, width), WIDE),
-            like((layers, pairs, width), WIDE),
-        ),
-        in_specs=[VMEM] * 4,
-        out_specs=[VMEM] * 6,
-        compiler_params=room(20),
+        out_shape=[pltpu.HBM(*a) for a in shapes],
+        in_specs=[FAR] * 4,
+        out_specs=[FAR] * 6,
+        scratch_shapes=[pltpu.VMEM(a.shape, LOW) for a in (pair, t_gate, t_up, t_down)]
+        + [pltpu.VMEM(*a) for a in shapes]
+        + [pltpu.SemaphoreType.DMA((4,)), pltpu.SemaphoreType.DMA((layers, 6))],
+        compiler_params=room(24),
         name="pair_forward",
-    )(pair, t_gate, t_up, t_down)
-
-
-def backward_kernel(
-    core, packed, spread, normed, inv, turned, hidden_t, by_gate, by_up, t_gate, t_up, t_down,
-    d_pair, kept, sent, wide_rows, grad_top,
-):
+    )(*far_away(pair, t_gate, t_up, t_down))
+
+
+def backward_kernel(core, packed, spread_far, *refs):
+    far, (d_pair, kept, sent), refs = refs[:9], refs[9:12], refs[12:]
+    near, (spread, wide_rows, grad_top, sems, spread_sem) = refs[:9], refs[9:]
+    normed, inv, turned, hidden_t, by_gate, by_up, t_gate, t_up, t_down = near
+    first = started([(spread_far, spread)], spread_sem)
+    arrived = {}
+    for layer in reversed(range(normed.shape[0])):
+        pairs = [(far[k].at[layer], near[k].at[layer]) for k in (3, 8, 4, 5, 2, 6, 7, 0, 1)]
+        arrived[layer] = started(pairs, sems.at[layer])
     heads = packed.shape[0]
     channels = normed.shape[2]
     rows = cols = math.isqrt(normed.shape[1])
@@ -206,6 +280,7 @@
         piece = packed[:, :, q * cols : (q + 1) * cols].astype(WIDE)
         for h in range(heads):
             wide_rows[h * rows + q * group : h * rows + (q + 1) * group, 0:cols] = piece[h]
+    waited(first)
     per_dot = LANES // heads
     for block in range(rows // per_dot):
         picked = jnp.concatenate(
@@ -217,16 +292,17 @@
         )
         top = nn(picked.T[0:cols].astype(LOW), spread[...])
         for i in range(per_dot):
-            first = (block * per_dot + i) * cols
-            grad_top[first : first + cols, :] = top[:, i * channels : (i + 1) * channels]
+            at = (block * per_dot + i) * cols
+            grad_top[at : at + cols, :] = top[:, i * channels : (i + 1) * channels]
     grad = grad_top[...]
     share = 1.0 / (heads * rows)
     for layer in reversed(range(normed.shape[0])):
         low = grad.astype(LOW)
+        waited(arrived[layer])
         down_sum = nn(hidden_t[layer], low)
         grad_hidden = nt(low, t_down[layer])
-        grad_gate = (grad_hidden * by_gate[layer]).astype(LOW)
-        grad_up = (grad_hidden * by_up[layer]).astype(LOW)
+        grad_gate = (grad_hidden * by_gate[layer].astype(WIDE)).astype(LOW)
+        grad_up = (grad_hidden * by_up[layer].astype(WIDE)).astype(LOW)
         gate_sum = nn(turned[layer], grad_gate)
         up_sum = nn(turned[layer], grad_up)
         for m, weight_sum in enumerate((gate_sum, up_sum, down_sum)):
@@ -261,15 +337,19 @@
     return pl.pallas_call(
         backward_kernel,
         out_shape=(like((pairs, channels), LOW), half, half),
-        in_specs=[SMEM] + [VMEM] * 11,
+        in_specs=[SMEM, VMEM] + [FAR] * 10,
         out_specs=[VMEM] * 3,
-        scratch_shapes=[
+        scratch_shapes=[pltpu.VMEM(a.shape, a.dtype) for a in (*saved, t_gate, t_up, t_down)]
+        + [
+            pltpu.VMEM(spread.shape, LOW),
             pltpu.VMEM((heads * rows, LANES), WIDE),
             pltpu.VMEM((pairs, channels), WIDE),
+            pltpu.SemaphoreType.DMA((t_gate.shape[0], 9)),
+            pltpu.SemaphoreType.DMA((1,)),
         ],
         compiler_params=room(20),
         name="pair_backward",
-    )(core, grad_rows, spread, *saved, t_gate, t_up, t_down)
+    )(core, grad_rows, *far_away(spread, *saved, t_gate, t_up, t_down))
 
 
 def exchange(pieces, axes):
@@ -292,29 +372,69 @@
     return jnp.broadcast_to(block, (count, *block.shape))
 
 
-def sum_everywhere(kept, sent):
+def finish_kernel(core, half, other, d_gate, d_up, d_down):
+    def fill(layer, source):
+        gate, up, down = (source[:, m].astype(WIDE).reshape(256, LANES) for m in range(3))
+        d_gate[layer] = jnp.concatenate([gate[:LANES], gate[LANES:]], axis=1)
+        d_up[layer] = jnp.concatenate([up[:LANES], up[LANES:]], axis=1)
+        d_down[layer] = down
+
+    for layer in range(2):
+
+        @pl.when(core[0] == layer)
+        def _(layer=layer):
+            fill(layer, half)
+            fill(1 - layer, other)
+
+
+def finish(core, half, other):
+    return pl.pallas_call(
+        finish_kernel,
+        out_shape=[like((2, 128, 256), WIDE), like((2, 128, 256), WIDE), like((2, 256, 128), WIDE)],
+        in_specs=[SMEM] + [VMEM] * 2,
+        out_specs=[VMEM] * 3,
+        compiler_params=room(8),
+        name="finish",
+    )(core, half, other)
+
+
+def sum_everywhere(core, kept, sent):
     half = added(kept, flipped(sent, "core", 1))
     block = summed(exchange(half, PLANE))
     block = summed(exchange(copies(block, 8), "z"))
     half = exchange(copies(block, 16), PLANE)
     other = flipped(half, "core", 1)
-    second = lax.axis_index("core") == 1
-    layers = jnp.stack([jnp.where(second, other, half), jnp.where(second, half, other)])
-    layers = layers.astype(WIDE).reshape(2, 16, 3, 16, LANES)
-    gate, up, down = (layers[:, :, m].reshape(2, 256, LANES) for m in range(3))
-
-    def wide(a):
-        return a.reshape(2, 2, 128, LANES).transpose(0, 2, 1, 3).reshape(2, 128, 256)
-
-    return wide(gate), wide(up), down
+    return finish(core, half.reshape(16, 3, 16, LANES), other.reshape(16, 3, 16, LANES))
+
+
+def halve_kernel(kept, received, near, away):
+    half = near.shape[0]
+    for k in range(2 * half):
+        total = (kept[k].astype(WIDE) + received[k].astype(WIDE)).astype(LOW)
+        if k < half:
+            near[k] = total
+        else:
+            away[k - half] = total
+
+
+def halve(kept, received):
+    half = like((kept.shape[0] // 2, *kept.shape[1:]), LOW)
+    return pl.pallas_call(
+        halve_kernel,
+        out_shape=(half, half),
+        in_specs=[VMEM] * 2,
+        out_specs=[VMEM] * 2,
+        compiler_params=room(8),
+        name="halve",
+    )(kept, received)
 
 
 def token_sum(kept, sent):
-    piece = added(kept, flipped(sent, "yl", 1))
+    received = flipped(sent, "yl", 1)
     for bit in (1, 2, 4):
-        count = piece.shape[0] // 2
-        piece = added(piece[:count], flipped(piece[count:], "z", bit))
-    return piece[0]
+        kept, sent = halve(kept, received)
+        received = flipped(sent, "z", bit)
+    return kept[0], received[0]
 
 
 def per_device(
@@ -349,10 +469,12 @@
     spread = jnp.einsum("ij,ch->ihjc", jnp.eye(per_dot, dtype=LOW), w_bias)
     spread = spread.reshape(LANES, per_dot * channels)
     grad_rows = exchange(bias_rows(received), HEAD)
-    d_tokens = token_sum(kept, sent)
+    piece, received = token_sum(kept, sent)
     d_pair, own, other = backward(core, grad_rows, spread, saved, t_gate, t_up, t_down)
-    d_gate, d_up, d_down = sum_everywhere(own.reshape(16, 48, LANES), other.reshape(16, 48, LANES))
-    return (d_tokens.transpose(0, 2, 1), d_pair.reshape(rows, cols, channels), d_gate, d_up, d_down)
+    sums = sum_everywhere(core, own.reshape(16, 48, LANES), other.reshape(16, 48, LANES))
+    received, *sums = lax.optimization_barrier((received, *sums))
+    d_tokens = added(piece, received).transpose(0, 2, 1)
+    return (d_tokens, d_pair.reshape(rows, cols, channels), *sums)
 
 
 def solution(mesh):

time: 126 us -> 105 us (0.83)
  local copies, waits for them, and re-layouts: 24.5 us -> 1.47 us
  Pallas kernels: 16.4 us -> 24.7 us
  starting transfers between devices: 35.5 us -> 31.8 us
  other arithmetic: 3.26 us -> 1.63 us
  blocking collectives: 14 us -> 15.4 us
  waiting for transfers between devices: 29.6 us -> 28.3 us
    unnamed x55 -> x3, local copies, waits for them, and re-layouts: 22.2 us -> 0.76 us
    pallas_call x2 -> x6, Pallas kernels: 6.79 us -> 12.5 us  [the longest x1 6.63 us: attend(): pl.pallas_call(attend_kernel, out_shape=(pltpu.HBM((length, length), LOW)...]
    all_to_all x4, waiting for transfers between devices: 23.3 us -> 17.7 us  [exchange(): return lax.all_to_all(pieces, axes, 0, 0, tiled=True)]
    ppermute x6, starting transfers between devices: 8.42 us -> 3.38 us  [flipped(): lax.ppermute(array, axis, [(k, k ^ bit) for k in range(lax.axis_size(axis...]
    ppermute x6, waiting for transfers between devices: 6.24 us -> 10.6 us  [flipped(): lax.ppermute(array, axis, [(k, k ^ bit) for k in range(lax.axis_size(axis...]
    convert_element_type x4 -> x1, other arithmetic: 2.28 us -> 0.74 us  [added(): return (kept.astype(WIDE) + received.astype(WIDE)).astype(LOW)]
    pallas_call x1, Pallas kernels: 5.01 us -> 6.46 us  [backward(): pl.pallas_call(backward_kernel, out_shape=(like((pairs, channels), LOW),...]
    all_to_all x4, starting transfers between devices: 27.1 us -> 28.5 us  [exchange(): return lax.all_to_all(pieces, axes, 0, 0, tiled=True)]
  transfers between devices with their start and end apart: 10 -> 10, of which waited for: 5 -> 7; matrix products, arithmetic and copies ran while one was open for 3% -> 2% of each run, Pallas kernels for 6% -> 17%
where the time goes in v3:
time: 105 us
  starting transfers between devices  31.8 us (30%)
  waiting for transfers between devices  28.3 us (27%)
  Pallas kernels  24.7 us (24%)
  blocking collectives  15.4 us (15%)
  other arithmetic  1.63 us (2%)
  local copies, waits for them, and re-layouts  1.47 us (1%)
  between operations  1.39 us (1%)
    all_to_all x4, starting transfers between devices, exchange(): return lax.all_to_all(pieces, axes, 0, 0, tiled=True)  28.5 us
    all_to_all x4, waiting for transfers between devices, exchange(): return lax.all_to_all(pieces, axes, 0, 0, tiled=True)  17.7 us
    all_to_all x1, blocking collectives, exchange(): return lax.all_to_all(pieces, axes, 0, 0, tiled=True)  15.4 us
    ppermute x6, waiting for transfers between devices, flipped(): lax.ppermute(array, axis, [(k, k ^ bit) for k in range(lax.axis_size(axis...  10.6 us
    pallas_call x1, Pallas kernels, attend(): pl.pallas_call(attend_kernel, out_shape=(pltpu.HBM((length, length), LOW)...  6.63 us
    pallas_call x1, Pallas kernels, backward(): pl.pallas_call(backward_kernel, out_shape=(like((pairs, channels), LOW),...  6.46 us
    pallas_call x1, Pallas kernels, token_pieces(): pl.pallas_call(token_kernel, out_shape=(half, half), in_specs=[SMEM] + [V...  4.88 us
    pallas_call x1, Pallas kernels, forward(): pl.pallas_call(forward_kernel, out_shape=[pltpu.HBM(*a) for a in shapes],...  4.58 us
  transfers between devices with their start and end apart: 10, of which 7 were waited for; matrix products, arithmetic and copies ran while one was open for 2% of the time, Pallas kernels for 17%

profile of v3, /device:TPU:2, one launch (start us, length us, event | category | flops | bytes accessed | tf_op | source)
XLA Modules:
  0.0 104.7 jit_solution(11827296643223120894)
XLA Ops:
  1.3 6.6 %attend.1 = (bf16[512,512]{1,0:T(8,128)(2,1)}, bf16[2,512,512]{2,1,0:T(8,128)(2,1)S(1)}, bf16[2,512,512]{2,1,0:T(8,128)(2,1)S(1)}, bf16[2,48,512]{2,1,0:T(8,128)...) custom-call(s32[1]{0:T(128)S(6)} %copy.21.valid, bf16[2,512,768]{2,1,0:T(8,128)(2,1)} %tokens_far.1, ...), custom_call_target="tpu_custom_call" | custom-call | tf_op jit(solution)/shard_map/attend/pallas_call | solution.py:122
  7.9 7.5 %all-to-all-start = ((bf16[16,32,512]{2,1,0:T(8,128)(2,1)}), bf16[16,32,512]{2,1,0:T(8,128)(2,1)S(1)}, u32[]{:S(2)}, u32[]{:S(2)}) async-start(bf16[16,32,512]{2,1,0:T(8,128)(2,1)} %bitcast.34), calls=%async_computation | async-start | bytes 1048576 | tf_op jit(solution)/shard_map/all_to_all | solution.py:356
  15.4 0.1 pad_add_fusion.place
  15.5 0.0 copy-start
  15.5 4.9 %token_pieces.1 = (bf16[8,2,48,512]{3,2,1,0:T(8,128)(2,1)S(1)}, bf16[8,2,48,512]{3,2,1,0:T(8,128)(2,1)}) custom-call(s32[2]{0:T(128)S(1)} %pad_add_fusion.place, bf16[2,512,512]{2,1,0:T(8,128)(2,1)S(1)} %get-tuple-element.35.dscores, bf16[2,512,512]{2,1,0:T(8,128)(2,1)S(1)} %get-tuple-element.36.probs, bf16[2,48,512]{2,1,0:T(8,128)(2,1)} %get-tuple-element.37.refs_0_, ...), custom_call_target="tpu_custom_call" | custom-call | tf_op jit(solution)/shard_map/token_pieces/pallas_call | solution.py:172
  20.4 0.8 collective-permute-start
  21.1 2.9 %all-to-all-done.pieces = bf16[16,32,512]{2,1,0:T(8,128)(2,1)S(1)} async-done(((bf16[16,32,512]{2,1,0:T(8,128)(2,1)}), bf16[16,32,512]{2,1,0:T(8,128)(2,1)S(1)}, u32[]{:S(2)}, u32[]{:S(2)}) %all-to-all-start) | async-done | bytes 524320 | tf_op jit(solution)/shard_map/all_to_all | solution.py:356
  24.0 0.9 bias_rows_sum.1
  24.9 8.7 %all-to-all-start.1 = ((bf16[16,8,128]{2,1,0:T(8,128)(2,1)}), bf16[16,8,128]{2,1,0:T(8,128)(2,1)S(1)}, u32[]{:S(2)}, u32[]{:S(2)}) async-start(bf16[16,8,128]{2,1,0:T(8,128)(2,1)} %bias_rows_sum.1), calls=%async_computation.1 | async-start | bytes 65536 | tf_op jit(solution)/shard_map/all_to_all | solution.py:356
  33.6 0.0 copy-done
  33.6 0.1 broadcast_multiply_fusion
  33.7 0.8 copy.20
  34.5 4.6 %pair_forward.1 = (f32[2,1024,128]{2,1,0:T(8,128)}, f32[2,1024,128]{2,1,0:T(8,128)}, bf16[2,128,1024]{2,1,0:T(8,128)(2,1)}, bf16[2,256,1024]{2,1,0:T(8,128)(2,1)...) custom-call(bf16[1024,128]{1,0:T(8,128)(2,1)} %bitcast.41, bf16[2,128,256]{2,1,0:T(8,128)(2,1)} %refs_6_.1, ...), custom_call_target="tpu_custom_call" | custom-call | tf_op jit(solution)/shard_map/pair_forward/pallas_call | solution.py:253
  39.0 3.1 %all-to-all-done.1.packed = bf16[16,8,128]{2,1,0:T(8,128)(2,1)S(1)} async-done(((bf16[16,8,128]{2,1,0:T(8,128)(2,1)}), bf16[16,8,128]{2,1,0:T(8,128)(2,1)S(1)}, u32[]{:S(2)}, u32[]{:S(2)}) %all-to-all-start.1) | async-done | bytes 32800 | tf_op jit(solution)/shard_map/all_to_all | solution.py:356
  42.1 6.5 %pair_backward.1 = (bf16[1024,128]{1,0:T(8,128)(2,1)}, bf16[16,3,16,128]{3,2,1,0:T(8,128)(2,1)S(1)}, bf16[16,3,16,128]{3,2,1,0:T(8,128)(2,1)S(1)}) custom-call(s32[1]{0:T(128)} %bitcast.8.core, bf16[16,8,128]{2,1,0:T(8,128)(2,1)S(1)} %all-to-all-done.1.packed, bf16[128,1024]{1,0:T(8,128)(2,1)} %bitcast.31, f32[2,1024,128]{2,1,0:T(8,128)} %get-tuple-element.49.refs_0_, ...), custom_call_target="tpu_custom_call" | custom-call | tf_op jit(solution)/shard_map/pair_backward/pallas_call | solution.py:337
  48.6 0.1 collective-permute-start.4
  48.7 1.4 %collective-permute-done.4 = bf16[16,48,128]{2,1,0:T(8,128)(2,1)S(1)} collective-permute-done((bf16[16,48,128]{2,1,0:T(8,128)(2,1)S(1)}, bf16[16,48,128]{2,1,0:T(8,128)(2,1)S(1)}, u32[]{:S(2)}, u32[]{:S(2)}) %collective-permute-start.4) | collective-permute-done | bytes 196640 | tf_op jit(solution)/shard_map/ppermute | solution.py:364
  50.1 0.7 fusion
  50.9 7.1 %all-to-all-start.2 = ((bf16[16,48,128]{2,1,0:T(8,128)(2,1)}), bf16[16,48,128]{2,1,0:T(8,128)(2,1)S(1)}, u32[]{:S(2)}, u32[]{:S(2)}) async-start(bf16[16,48,128]{2,1,0:T(8,128)(2,1)} %fusion), calls=%async_computation.2 | async-start | bytes 393216 | tf_op jit(solution)/shard_map/all_to_all | solution.py:356
  58.0 0.0 collective-permute-done.received
  58.0 0.2 halve.3
  58.2 0.9 collective-permute-start.1
  59.1 5.8 %all-to-all-done.2 = bf16[16,48,128]{2,1,0:T(8,128)(2,1)S(1)} async-done(((bf16[16,48,128]{2,1,0:T(8,128)(2,1)}), bf16[16,48,128]{2,1,0:T(8,128)(2,1)S(1)}, u32[]{:S(2)}, u32[]{:S(2)}) %all-to-all-start.2) | async-done | bytes 196640 | tf_op jit(solution)/shard_map/all_to_all | solution.py:356
  64.9 15.4 %all_to_all.25 = bf16[8,48,128]{2,1,0:T(8,128)(2,1)S(1)} all-to-all(bf16[8,48,128]{2,1,0:T(8,128)(2,1)S(1)} %broadcast_in_dim.6), channel_id=1, replica_groups=mesh['yh'=2,'x'=4,'core'=2,'yl'=2,'z'=8] {'z'}, dimensions={0} | all-to-all | bytes 196608 | tf_op jit(solution)/shard_map/all_to_all | solution.py:356
  80.3 0.7 broadcast_in_dim.7
  81.0 5.2 %all-to-all-start.4 = ((bf16[16,48,128]{2,1,0:T(8,128)(2,1)}), bf16[16,48,128]{2,1,0:T(8,128)(2,1)S(1)}, u32[]{:S(2)}, u32[]{:S(2)}) async-start(bf16[16,48,128]{2,1,0:T(8,128)(2,1)} %broadcast_in_dim.7), calls=%async_computation.4 | async-start | bytes 393216 | tf_op jit(solution)/shard_map/all_to_all | solution.py:356
  86.2 0.0 collective-permute-done.1.received
  86.2 0.1 halve.4
  86.3 0.5 collective-permute-start.2
  86.8 6.0 %all-to-all-done.4 = bf16[16,48,128]{2,1,0:T(8,128)(2,1)S(1)} async-done(((bf16[16,48,128]{2,1,0:T(8,128)(2,1)}), bf16[16,48,128]{2,1,0:T(8,128)(2,1)S(1)}, u32[]{:S(2)}, u32[]{:S(2)}) %all-to-all-start.4) | async-done | bytes 196640 | tf_op jit(solution)/shard_map/all_to_all | solution.py:356
  92.8 0.0 collective-permute-start.5
  92.8 2.4 %collective-permute-done.2.received = bf16[2,2,48,512]{3,2,1,0:T(8,128)(2,1)S(1)} collective-permute-done((bf16[2,2,48,512]{3,2,1,0:T(8,128)(2,1)S(1)}, bf16[2,2,48,512]{3,2,1,0:T(8,128)(2,1)S(1)}, u32[]{:S(2)}, u32[]{:S(2)}) %collective-permute-start.2) | collective-permute-done | bytes 196640 | tf_op jit(solution)/shard_map/ppermute | solution.py:364
  95.3 1.1 %collective-permute-start.3 = (bf16[1,2,48,512]{3,2,1,0:T(8,128)(2,1)S(1)}, bf16[1,2,48,512]{3,2,1,0:T(8,128)(2,1)S(1)}, u32[]{:S(2)}, u32[]{:S(2)}) collective-permute-start(bf16[1,2,48,512]{3,2,1,0:T(8,128)(2,1)S(1)} %get-tuple-element.47), channel_id=1, source_target_pairs={{0,4},{1,5},{2,6},{3,7},{4,0},{5,1},{6,2},{7,3},{8,12},{9,13},{10,... | collective-permute-start | bytes 294920 | tf_op jit(solution)/shard_map/ppermute | solution.py:364
  96.3 0.0 collective-permute-done.5
  96.3 0.9 finish.1
  97.3 6.8 %collective-permute-done.3 = bf16[1,2,48,512]{3,2,1,0:T(8,128)(2,1)S(1)} collective-permute-done((bf16[1,2,48,512]{3,2,1,0:T(8,128)(2,1)S(1)}, bf16[1,2,48,512]{3,2,1,0:T(8,128)(2,1)S(1)}, u32[]{:S(2)}, u32[]{:S(2)}) %collective-permute-start.3) | collective-permute-done | bytes 98336 | tf_op jit(solution)/shard_map/ppermute | solution.py:364
  104.0 0.7 fusion.2
  (5 shorter events, 0.1 us)
Async XLA Ops:
  7.9 16.1 %all-to-all-start = ((bf16[16,32,512]{2,1,0:T(8,128)(2,1)}), bf16[16,32,512]{2,1,0:T(8,128)(2,1)S(1)}, u32[]{:S(2)}, u32[]{:S(2)}) async-start(bf16[16,32,512]{2,1,0:T(8,128)(2,1)} %bitcast.34), calls=%async_computation | async-start | bytes 1048576 | tf_op jit(solution)/shard_map/all_to_all | solution.py:356
  15.5 18.1 %copy-start = (bf16[128,16]{0,1:T(8,128)(2,1)S(1)}, bf16[128,16]{0,1:T(8,128)(2,1)}, u32[]{:S(2)}) copy-start(bf16[128,16]{0,1:T(8,128)(2,1)} %param.22) | copy-start | bytes 12292
  20.4 37.6 %collective-permute-start = (bf16[8,2,48,512]{3,2,1,0:T(8,128)(2,1)}, bf16[8,2,48,512]{3,2,1,0:T(8,128)(2,1)S(1)}, u32[]{:S(2)}, u32[]{:S(2)}) collective-permute-start(bf16[8,2,48,512]{3,2,1,0:T(8,128)(2,1)} %get-tuple-element.41), channel_id=1, source_target_pairs={{0,8},{8,0},{1,9},{9,1},{2,10},{10,2},{3,11},{11,3},{4,12},{12,4},... | collective-permute-start | bytes 2359304 | tf_op jit(solution)/shard_map/ppermute | solution.py:364
  24.9 17.2 %all-to-all-start.1 = ((bf16[16,8,128]{2,1,0:T(8,128)(2,1)}), bf16[16,8,128]{2,1,0:T(8,128)(2,1)S(1)}, u32[]{:S(2)}, u32[]{:S(2)}) async-start(bf16[16,8,128]{2,1,0:T(8,128)(2,1)} %bias_rows_sum.1), calls=%async_computation.1 | async-start | bytes 65536 | tf_op jit(solution)/shard_map/all_to_all | solution.py:356
  48.6 1.5 %collective-permute-start.4 = (bf16[16,48,128]{2,1,0:T(8,128)(2,1)S(1)}, bf16[16,48,128]{2,1,0:T(8,128)(2,1)S(1)}, u32[]{:S(2)}, u32[]{:S(2)}) collective-permute-start(bf16[16,48,128]{2,1,0:T(8,128)(2,1)S(1)} %bitcast.30), channel_id=1, source_target_pairs={{0,16},{16,0},{1,17},{17,1},{2,18},{18,2},{3,19},{19,3},{4,20},{20... | collective-permute-start | bytes 589832 | tf_op jit(solution)/shard_map/ppermute | solution.py:364
  50.9 14.0 %all-to-all-start.2 = ((bf16[16,48,128]{2,1,0:T(8,128)(2,1)}), bf16[16,48,128]{2,1,0:T(8,128)(2,1)S(1)}, u32[]{:S(2)}, u32[]{:S(2)}) async-start(bf16[16,48,128]{2,1,0:T(8,128)(2,1)} %fusion), calls=%async_computation.2 | async-start | bytes 393216 | tf_op jit(solution)/shard_map/all_to_all | solution.py:356
  58.2 28.1 %collective-permute-start.1 = (bf16[4,2,48,512]{3,2,1,0:T(8,128)(2,1)S(1)}, bf16[4,2,48,512]{3,2,1,0:T(8,128)(2,1)S(1)}, u32[]{:S(2)}, u32[]{:S(2)}) collective-permute-start(bf16[4,2,48,512]{3,2,1,0:T(8,128)(2,1)S(1)} %get-tuple-element.43), channel_id=1, source_target_pairs={{0,1},{1,0},{2,3},{3,2},{4,5},{5,4},{6,7},{7,6},{8,9},{9,8},{10,11... | collective-permute-start | bytes 1179656 | tf_op jit(solution)/shard_map/ppermute | solution.py:364
  81.0 11.8 %all-to-all-start.4 = ((bf16[16,48,128]{2,1,0:T(8,128)(2,1)}), bf16[16,48,128]{2,1,0:T(8,128)(2,1)S(1)}, u32[]{:S(2)}, u32[]{:S(2)}) async-start(bf16[16,48,128]{2,1,0:T(8,128)(2,1)} %broadcast_in_dim.7), calls=%async_computation.4 | async-start | bytes 393216 | tf_op jit(solution)/shard_map/all_to_all | solution.py:356
  86.3 8.9 %collective-permute-start.2 = (bf16[2,2,48,512]{3,2,1,0:T(8,128)(2,1)S(1)}, bf16[2,2,48,512]{3,2,1,0:T(8,128)(2,1)S(1)}, u32[]{:S(2)}, u32[]{:S(2)}) collective-permute-start(bf16[2,2,48,512]{3,2,1,0:T(8,128)(2,1)S(1)} %get-tuple-element.45), channel_id=1, source_target_pairs={{0,2},{1,3},{2,0},{3,1},{4,6},{5,7},{6,4},{7,5},{8,10},{9,11},{10,... | collective-permute-start | bytes 589832 | tf_op jit(solution)/shard_map/ppermute | solution.py:364
  92.8 3.5 %collective-permute-start.5 = (bf16[16,48,128]{2,1,0:T(8,128)(2,1)S(1)}, bf16[16,48,128]{2,1,0:T(8,128)(2,1)S(1)}, u32[]{:S(2)}, u32[]{:S(2)}) collective-permute-start(bf16[16,48,128]{2,1,0:T(8,128)(2,1)S(1)} %all-to-all-done.4), channel_id=1, source_target_pairs={{0,16},{16,0},{1,17},{17,1},{2,18},{18,2},{3,19},{19,3},{4,20},{20... | collective-permute-start | bytes 589832 | tf_op jit(solution)/shard_map/ppermute | solution.py:364
  95.3 8.8 %collective-permute-start.3 = (bf16[1,2,48,512]{3,2,1,0:T(8,128)(2,1)S(1)}, bf16[1,2,48,512]{3,2,1,0:T(8,128)(2,1)S(1)}, u32[]{:S(2)}, u32[]{:S(2)}) collective-permute-start(bf16[1,2,48,512]{3,2,1,0:T(8,128)(2,1)S(1)} %get-tuple-element.47), channel_id=1, source_target_pairs={{0,4},{1,5},{2,6},{3,7},{4,0},{5,1},{6,2},{7,3},{8,12},{9,13},{10,... | collective-permute-start | bytes 294920 | tf_op jit(solution)/shard_map/ppermute | solution.py:364

commit v4 on v3

--- a/solution.py
+++ b/solution.py
@@ -82,15 +82,15 @@
         ],
         sems,
     )
-    key_rows, value_rows = [], []
+    rows = []
     for s in range(samples):
-        waited(moves[:6] if s == 0 else moves[6:8])
+        waited(moves[:4] if s == 0 else moves[6:7])
         x = tokens[s]
-        queries[s] = nt(wq[...], x).astype(LOW)
-        keys[s] = nt(wk[...], x).astype(LOW)
-        grads[s] = nt(wo[...], cotangent[s]).astype(LOW)
-        key_rows.append(nt(x, wk[...]).astype(LOW))
-        value_rows.append(nt(x, wv[...]).astype(LOW))
+        query, key, value = (nt(x, w[...]).astype(LOW) for w in (wq, wk, wv))
+        waited(moves[4:6] if s == 0 else moves[7:8])
+        grad = nt(cotangent[s], wo[...]).astype(LOW)
+        queries[s], keys[s], grads[s] = query, key, grad
+        rows.append((key, value))
     leaving = started(
         [(queries, queries_far), (keys, keys_far), (grads, grads_far)], out_sems.at[0]
     )
@@ -101,11 +101,11 @@
         turned = jnp.where(kept, bias[block, :].astype(WIDE).T, MASKED)
         total = None
         for s in range(samples):
-            scores = nn(key_rows[s], queries[s, :, block]) * scale + turned
+            scores = nt(rows[s][0], queries[s, block, :]) * scale + turned
             exps = jnp.exp(scores - jnp.max(scores, axis=0, keepdims=True))
             prob = exps * (1.0 / jnp.sum(exps, axis=0, keepdims=True))
             probs[s, :, block] = prob.astype(LOW)
-            grad_prob = nn(value_rows[s], grads[s, :, block])
+            grad_prob = nt(rows[s][1], grads[s, block, :])
             mean = jnp.sum(prob * grad_prob, axis=0, keepdims=True)
             dscore = prob * (grad_prob - mean)
             dscores[s, :, block] = dscore.astype(LOW)
@@ -118,7 +118,7 @@
 def attend(valid, tokens, cotangent, wq, wk, wv, wo, bias):
     samples, length, _ = tokens.shape
     square = like((samples, length, length), LOW)
-    heads = pltpu.HBM((samples, HD, length), LOW)
+    heads = pltpu.HBM((samples, length, HD), LOW)
     return pl.pallas_call(
         attend_kernel,
         out_shape=(pltpu.HBM((length, length), LOW), square, square, heads, heads, heads),
@@ -128,7 +128,7 @@
             pltpu.VMEM(a.shape, LOW) for a in (tokens, cotangent, wq, wk, wv, wo, bias)
         ]
         + [pltpu.VMEM((length, length), LOW)]
-        + [pltpu.VMEM((samples, HD, length), LOW)] * 3
+        + [pltpu.VMEM((samples, length, HD), LOW)] * 3
         + [pltpu.SemaphoreType.DMA((9,)), pltpu.SemaphoreType.DMA((2, 4))],
         compiler_params=room(16),
         name="attend",
@@ -145,9 +145,9 @@
         d = dscores[s]
         joined = jnp.concatenate(
             [
-                (nn(keys[s], d) * scale).astype(LOW),
-                (nt(queries[s], d) * scale).astype(LOW),
-                nt(grads[s], probs[s]).astype(LOW),
+                (nn(keys[s].T, d) * scale).astype(LOW),
+                (nt(queries[s].T, d) * scale).astype(LOW),
+                nt(grads[s].T, probs[s]).astype(LOW),
             ],
             axis=0,
         )
@@ -168,7 +168,7 @@
 
 def token_pieces(place, dscores, probs, queries, keys, grads, wq, wk, wv):
     samples, length, _ = dscores.shape
-    half = like((8, samples, HD, length), LOW)
+    half = pltpu.HBM((8, samples, HD, length), LOW)
     return pl.pallas_call(
         token_kernel,
         out_shape=(half, half),
@@ -202,86 +202,134 @@
     )(pieces)
 
 
-def forward_kernel(pair_far, t_gate_far, t_up_far, t_down_far, *refs):
-    far, (pair, t_gate, t_up, t_down, *near, in_sems, out_sems) = refs[:6], refs[6:]
-    normed, inv, turned, hidden_t, by_gate, by_up = near
-    layers = t_gate.shape[0]
-    moves = started(
-        [(pair_far, pair), (t_gate_far, t_gate), (t_up_far, t_up), (t_down_far, t_down)], in_sems
-    )
+def forward_step(field, gate_weight, up_weight):
+    centred = field - jnp.mean(field, axis=-1, keepdims=True)
+    variance = jnp.mean(centred * centred, axis=-1, keepdims=True)
+    inv_std = lax.rsqrt(variance + EPS_NORM)
+    unit = centred * inv_std
+    low = unit.astype(LOW)
+    gate = nn(low, gate_weight)
+    up = nn(low, up_weight)
+    sig = jax.nn.sigmoid(gate)
+    act = gate * sig
+    hidden = (act * up).astype(LOW)
+    saved = (
+        unit,
+        jnp.broadcast_to(inv_std, unit.shape),
+        low.T,
+        hidden.T,
+        (up * (sig * (1.0 + gate * (1.0 - sig)))).astype(LOW),
+        act.astype(LOW),
+    )
+    return saved, hidden
+
+
+def first_kernel(pair_far, t_gate_far, t_up_far, t_down_far, *refs):
+    far, (pair, t_gate, t_up, t_down, *near, in_sems, out_sems) = refs[:7], refs[7:]
+    waited(
+        started(
+            [
+                (pair_far, pair),
+                (t_gate_far.at[0], t_gate),
+                (t_up_far.at[0], t_up),
+                (t_down_far.at[0], t_down),
+            ],
+            in_sems,
+        )
+    )
+    field = pair[...].astype(WIDE)
+    saved, hidden = forward_step(field, t_gate[...], t_up[...])
+    for ref, value in zip(near, saved):
+        ref[...] = value
+    moves = started(list(zip(near[:6], far[:6])), out_sems)
+    near[6][...] = field + nn(hidden, t_down[...])
+    waited(moves + started([(near[6], far[6])], out_sems.at[6:]))
+
+
+def second_kernel(field_far, t_gate_far, t_up_far, *refs):
+    far, out, (field, t_gate, t_up, *near, in_sems, out_sems) = refs[:2], refs[2:6], refs[6:]
+    waited(
+        started(
+            [(field_far, field), (t_gate_far.at[1], t_gate), (t_up_far.at[1], t_up)], in_sems
+        )
+    )
+    saved, _ = forward_step(field[...], t_gate[...], t_up[...])
+    for ref, value in zip((*near, *out), saved):
+        ref[...] = value
+        if ref is near[1]:
+            moves = started(list(zip(near, far)), out_sems)
     waited(moves)
-    field = pair[...].astype(WIDE)
-    moves = []
-    for layer in range(layers):
-        centred = field - jnp.mean(field, axis=-1, keepdims=True)
-        variance = jnp.mean(centred * centred, axis=-1, keepdims=True)
-        inv_std = lax.rsqrt(variance + EPS_NORM)
-        unit = centred * inv_std
-        low = unit.astype(LOW)
-        gate = nn(low, t_gate[layer])
-        up = nn(low, t_up[layer])
-        sig = jax.nn.sigmoid(gate)
-        act = gate * sig
-        hidden = (act * up).astype(LOW)
-        normed[layer] = unit
-        inv[layer] = jnp.broadcast_to(inv_std, unit.shape)
-        turned[layer] = low.T
-        hidden_t[layer] = hidden.T
-        by_gate[layer] = (up * (sig * (1.0 + gate * (1.0 - sig)))).astype(LOW)
-        by_up[layer] = act.astype(LOW)
-        pairs = [(a.at[layer], b.at[layer]) for a, b in zip(near, far)]
-        moves += started(pairs, out_sems.at[layer])
-        if layer + 1 < layers:
-            field = field + nn(hidden, t_down[layer])
-    waited(moves)
-
-
-def saved_shapes(pairs, channels, layers, width):
+
+
+def saved_shapes(pairs, channels, width):
     return (
-        ((layers, pairs, channels), WIDE),
-        ((layers, pairs, channels), WIDE),
-        ((layers, channels, pairs), LOW),
-        ((layers, width, pairs), LOW),
-        ((layers, pairs, width), LOW),
-        ((layers, pairs, width), LOW),
-    )
-
-
-def forward(pair, t_gate, t_up, t_down):
-    layers, _, width = t_gate.shape
-    shapes = saved_shapes(*pair.shape, layers, width)
-    return pl.pallas_call(
-        forward_kernel,
+        ((pairs, channels), WIDE),
+        ((pairs, channels), WIDE),
+        ((channels, pairs), LOW),
+        ((width, pairs), LOW),
+        ((pairs, width), LOW),
+        ((pairs, width), LOW),
+    )
+
+
+def forward_first(pair, t_gate, t_up, t_down):
+    shapes = (*saved_shapes(*pair.shape, t_gate.shape[2]), (pair.shape, WIDE))
+    *saved, field = pl.pallas_call(
+        first_kernel,
         out_shape=[pltpu.HBM(*a) for a in shapes],
         in_specs=[FAR] * 4,
-        out_specs=[FAR] * 6,
-        scratch_shapes=[pltpu.VMEM(a.shape, LOW) for a in (pair, t_gate, t_up, t_down)]
+        out_specs=[FAR] * 7,
+        scratch_shapes=[
+            pltpu.VMEM(a, LOW)
+            for a in (pair.shape, t_gate.shape[1:], t_up.shape[1:], t_down.shape[1:])
+        ]
         + [pltpu.VMEM(*a) for a in shapes]
-        + [pltpu.SemaphoreType.DMA((4,)), pltpu.SemaphoreType.DMA((layers, 6))],
+        + [pltpu.SemaphoreType.DMA((4,)), pltpu.SemaphoreType.DMA((7,))],
         compiler_params=room(24),
-        name="pair_forward",
+        name="pair_forward_0",
     )(*far_away(pair, t_gate, t_up, t_down))
-
-
-def backward_kernel(core, packed, spread_far, *refs):
-    far, (d_pair, kept, sent), refs = refs[:9], refs[9:12], refs[12:]
-    near, (spread, wide_rows, grad_top, sems, spread_sem) = refs[:9], refs[9:]
-    normed, inv, turned, hidden_t, by_gate, by_up, t_gate, t_up, t_down = near
-    first = started([(spread_far, spread)], spread_sem)
-    arrived = {}
-    for layer in reversed(range(normed.shape[0])):
-        pairs = [(far[k].at[layer], near[k].at[layer]) for k in (3, 8, 4, 5, 2, 6, 7, 0, 1)]
-        arrived[layer] = started(pairs, sems.at[layer])
+    return saved, field
+
+
+def forward_second(field, t_gate, t_up):
+    shapes = saved_shapes(*field.shape, t_gate.shape[2])
+    return pl.pallas_call(
+        second_kernel,
+        out_shape=[pltpu.HBM(*a) for a in shapes[:2]] + [like(*a) for a in shapes[2:]],
+        in_specs=[FAR] * 3,
+        out_specs=[FAR] * 2 + [VMEM] * 4,
+        scratch_shapes=[
+            pltpu.VMEM(field.shape, WIDE),
+            pltpu.VMEM(t_gate.shape[1:], LOW),
+            pltpu.VMEM(t_up.shape[1:], LOW),
+            pltpu.VMEM(*shapes[0]),
+            pltpu.VMEM(*shapes[1]),
+            pltpu.SemaphoreType.DMA((3,)),
+            pltpu.SemaphoreType.DMA((2,)),
+        ],
+        compiler_params=room(16),
+        name="pair_forward_1",
+    )(*far_away(field, t_gate, t_up))
+
+
+def backward_kernel(core, packed, *refs):
+    last, far, (d_pair, kept, sent), refs = refs[:4], refs[4:16], refs[16:19], refs[19:]
+    near, (wide_rows, grad_top, spread, sems) = refs[:12], refs[12:]
+    w_bias, t_down, t_gate, t_up = near[:4]
+    moves = started(list(zip(far, near)), sems)
     heads = packed.shape[0]
-    channels = normed.shape[2]
-    rows = cols = math.isqrt(normed.shape[1])
+    pairs, channels = grad_top.shape
+    rows = cols = math.isqrt(pairs)
     group = packed.shape[1]
     for q in range(LANES // cols):
         piece = packed[:, :, q * cols : (q + 1) * cols].astype(WIDE)
         for h in range(heads):
             wide_rows[h * rows + q * group : h * rows + (q + 1) * group, 0:cols] = piece[h]
-    waited(first)
     per_dot = LANES // heads
+    spread[...] = jnp.zeros(spread.shape, LOW)
+    waited(moves[:1])
+    for i in range(per_dot):
+        spread[i * heads : (i + 1) * heads, i * channels : (i + 1) * channels] = w_bias[...]
     for block in range(rows // per_dot):
         picked = jnp.concatenate(
             [
@@ -296,15 +344,17 @@
             grad_top[at : at + cols, :] = top[:, i * channels : (i + 1) * channels]
     grad = grad_top[...]
     share = 1.0 / (heads * rows)
-    for layer in reversed(range(normed.shape[0])):
+    for layer in (1, 0):
+        normed, inv, turned, hidden_t, by_gate, by_up = (*near[4:6], *last) if layer else near[6:]
         low = grad.astype(LOW)
-        waited(arrived[layer])
-        down_sum = nn(hidden_t[layer], low)
+        waited(moves[1:2] if layer else moves[6:])
+        down_sum = nn(hidden_t[...], low)
         grad_hidden = nt(low, t_down[layer])
-        grad_gate = (grad_hidden * by_gate[layer].astype(WIDE)).astype(LOW)
-        grad_up = (grad_hidden * by_up[layer].astype(WIDE)).astype(LOW)
-        gate_sum = nn(turned[layer], grad_gate)
-        up_sum = nn(turned[layer], grad_up)
+        grad_gate = (grad_hidden * by_gate[...].astype(WIDE)).astype(LOW)
+        grad_up = (grad_hidden * by_up[...].astype(WIDE)).astype(LOW)
+        waited(moves[2:4] if layer else [])
+        gate_sum = nn(turned[...], grad_gate)
+        up_sum = nn(turned[...], grad_up)
         for m, weight_sum in enumerate((gate_sum, up_sum, down_sum)):
             if weight_sum.shape[1] != LANES:
                 weight_sum = jnp.concatenate(
@@ -321,8 +371,9 @@
                 sent[:, m] = weight_sum
 
         grad_normed = nt(grad_gate, t_gate[layer]) + nt(grad_up, t_up[layer])
-        unit = normed[layer]
-        grad = grad + inv[layer] * (
+        waited(moves[4:6] if layer else [])
+        unit = normed[...]
+        grad = grad + inv[...] * (
             grad_normed
             - jnp.mean(grad_normed, axis=-1, keepdims=True)
             - unit * jnp.mean(grad_normed * unit, axis=-1, keepdims=True)
@@ -330,26 +381,26 @@
     d_pair[...] = grad.astype(LOW)
 
 
-def backward(core, grad_rows, spread, saved, t_gate, t_up, t_down):
-    pairs, channels = saved[0].shape[1:]
+def backward(core, grad_rows, w_bias, first, last, t_gate, t_up, t_down):
+    pairs, channels = last[0].shape
     heads, rows = grad_rows.shape[0], math.isqrt(pairs)
     half = like((16, 3, 16, LANES), LOW)
+    far = (w_bias, t_down, t_gate, t_up, *last[:2], *first)
     return pl.pallas_call(
         backward_kernel,
         out_shape=(like((pairs, channels), LOW), half, half),
-        in_specs=[SMEM, VMEM] + [FAR] * 10,
+        in_specs=[SMEM] + [VMEM] * 5 + [FAR] * 12,
         out_specs=[VMEM] * 3,
-        scratch_shapes=[pltpu.VMEM(a.shape, a.dtype) for a in (*saved, t_gate, t_up, t_down)]
+        scratch_shapes=[pltpu.VMEM(a.shape, a.dtype) for a in far]
         + [
-            pltpu.VMEM(spread.shape, LOW),
             pltpu.VMEM((heads * rows, LANES), WIDE),
             pltpu.VMEM((pairs, channels), WIDE),
-            pltpu.SemaphoreType.DMA((t_gate.shape[0], 9)),
-            pltpu.SemaphoreType.DMA((1,)),
+            pltpu.VMEM((LANES, LANES // heads * channels), LOW),
+            pltpu.SemaphoreType.DMA((12,)),
         ],
         compiler_params=room(20),
         name="pair_backward",
-    )(core, grad_rows, *far_away(spread, *saved, t_gate, t_up, t_down))
+    )(core, grad_rows, *last[2:], *far_away(*far))
 
 
 def exchange(pieces, axes):
@@ -372,7 +423,7 @@
     return jnp.broadcast_to(block, (count, *block.shape))
 
 
-def finish_kernel(core, half, other, d_gate, d_up, d_down):
+def finish_kernel(core, half, other, piece, received, d_gate, d_up, d_down, d_tokens):
     def fill(layer, source):
         gate, up, down = (source[:, m].astype(WIDE).reshape(256, LANES) for m in range(3))
         d_gate[layer] = jnp.concatenate([gate[:LANES], gate[LANES:]], axis=1)
@@ -386,25 +437,32 @@
             fill(layer, half)
             fill(1 - layer, other)
 
-
-def finish(core, half, other):
+    d_tokens[...] = (piece[...].astype(WIDE) + received[...].astype(WIDE)).astype(LOW)
+
+
+def finish(core, half, other, piece, received):
     return pl.pallas_call(
         finish_kernel,
-        out_shape=[like((2, 128, 256), WIDE), like((2, 128, 256), WIDE), like((2, 256, 128), WIDE)],
-        in_specs=[SMEM] + [VMEM] * 2,
-        out_specs=[VMEM] * 3,
+        out_shape=[
+            like((2, 128, 256), WIDE),
+            like((2, 128, 256), WIDE),
+            like((2, 256, 128), WIDE),
+            like(piece.shape, LOW),
+        ],
+        in_specs=[SMEM] + [VMEM] * 4,
+        out_specs=[VMEM] * 4,
         compiler_params=room(8),
         name="finish",
-    )(core, half, other)
-
-
-def sum_everywhere(core, kept, sent):
+    )(core, half, other, piece, received)
+
+
+def sum_everywhere(kept, sent):
     half = added(kept, flipped(sent, "core", 1))
     block = summed(exchange(half, PLANE))
     block = summed(exchange(copies(block, 8), "z"))
     half = exchange(copies(block, 16), PLANE)
     other = flipped(half, "core", 1)
-    return finish(core, half.reshape(16, 3, 16, LANES), other.reshape(16, 3, 16, LANES))
+    return half.reshape(16, 3, 16, LANES), other.reshape(16, 3, 16, LANES)
 
 
 def halve_kernel(kept, received, near, away):
@@ -454,7 +512,6 @@
 ):
     tokens = input_tokens.shape[1]
     rows, cols, channels = pair_in.shape
-    heads = w_bias.shape[1]
     wq, wk, wv = query_weight.T, key_weight.T, value_weight.T
     core = lax.axis_index("core").reshape(1)
     z = lax.axis_index("z")
@@ -464,17 +521,14 @@
     )
     received = exchange(part.reshape(16, tokens // 16, tokens), SAMP)
     kept, sent = token_pieces(place, dscores, probs, queries, keys, grads, wq, wk, wv)
-    saved = forward(pair_in.reshape(rows * cols, channels), t_gate, t_up, t_down)
-    per_dot = LANES // heads
-    spread = jnp.einsum("ij,ch->ihjc", jnp.eye(per_dot, dtype=LOW), w_bias)
-    spread = spread.reshape(LANES, per_dot * channels)
+    first, field = forward_first(pair_in.reshape(rows * cols, channels), t_gate, t_up, t_down)
+    last = forward_second(field, t_gate, t_up)
     grad_rows = exchange(bias_rows(received), HEAD)
     piece, received = token_sum(kept, sent)
-    d_pair, own, other = backward(core, grad_rows, spread, saved, t_gate, t_up, t_down)
-    sums = sum_everywhere(core, own.reshape(16, 48, LANES), other.reshape(16, 48, LANES))
-    received, *sums = lax.optimization_barrier((received, *sums))
-    d_tokens = added(piece, received).transpose(0, 2, 1)
-    return (d_tokens, d_pair.reshape(rows, cols, channels), *sums)
+    d_pair, own, other = backward(core, grad_rows, w_bias.T, first, last, t_gate, t_up, t_down)
+    half, other = sum_everywhere(own.reshape(16, 48, LANES), other.reshape(16, 48, LANES))
+    *sums, d_tokens = finish(core, half, other, piece, received)
+    return (d_tokens.transpose(0, 2, 1), d_pair.reshape(rows, cols, channels), *sums)
 
 
 def solution(mesh):

time: 105 us -> 105 us (level)
  Pallas kernels: 24.7 us -> 26.3 us
    pallas_call x1 -> x2, Pallas kernels: 4.58 us -> 6.25 us  [the longest x1 3.47 us: forward_first(): pl.pallas_call(first_kernel, out_shape=[pltpu.HBM(*a) for a in shapes], i...]
    all_to_all x4, waiting for transfers between devices: 17.7 us -> 16.6 us  [exchange(): return lax.all_to_all(pieces, axes, 0, 0, tiled=True)]
    ppermute x6, waiting for transfers between devices: 10.6 us -> 11.7 us  [flipped(): lax.ppermute(array, axis, [(k, k ^ bit) for k in range(lax.axis_size(axis...]
where the time goes in v4:
time: 105 us
  starting transfers between devices  31.7 us (30%)
  waiting for transfers between devices  28.3 us (27%)
  Pallas kernels  26.3 us (25%)
  blocking collectives  15.6 us (15%)
  between operations  1.39 us (1%)
    all_to_all x4, starting transfers between devices, exchange(): return lax.all_to_all(pieces, axes, 0, 0, tiled=True)  28.5 us
    all_to_all x4, waiting for transfers between devices, exchange(): return lax.all_to_all(pieces, axes, 0, 0, tiled=True)  16.6 us
    all_to_all x1, blocking collectives, exchange(): return lax.all_to_all(pieces, axes, 0, 0, tiled=True)  15.6 us
    ppermute x6, waiting for transfers between devices, flipped(): lax.ppermute(array, axis, [(k, k ^ bit) for k in range(lax.axis_size(axis...  11.7 us
    pallas_call x1, Pallas kernels, attend(): pl.pallas_call(attend_kernel, out_shape=(pltpu.HBM((length, length), LOW)...  6.96 us
    pallas_call x1, Pallas kernels, backward(): pl.pallas_call(backward_kernel, out_shape=(like((pairs, channels), LOW),...  5.68 us
    pallas_call x1, Pallas kernels, token_pieces(): pl.pallas_call(token_kernel, out_shape=(half, half), in_specs=[SMEM] + [V...  5.22 us
    pallas_call x1, Pallas kernels, forward_first(): pl.pallas_call(first_kernel, out_shape=[pltpu.HBM(*a) for a in shapes], i...  3.47 us
  transfers between devices with their start and end apart: 10, of which 7 were waited for; matrix products, arithmetic and copies ran while one was open for 2% of the time, Pallas kernels for 17%

profile of v4, /device:TPU:2, one launch (start us, length us, event | category | flops | bytes accessed | tf_op | source)
XLA Modules:
  0.0 104.8 jit_solution(10289413872007892401)
XLA Ops:
  1.3 7.0 %attend.1 = (bf16[512,512]{1,0:T(8,128)(2,1)}, bf16[2,512,512]{2,1,0:T(8,128)(2,1)S(1)}, bf16[2,512,512]{2,1,0:T(8,128)(2,1)S(1)}, bf16[2,512,48]{2,1,0:T(8,128)...) custom-call(s32[1]{0:T(128)S(6)} %copy.18.valid, bf16[2,512,768]{2,1,0:T(8,128)(2,1)} %tokens_far.1, ...), custom_call_target="tpu_custom_call" | custom-call | tf_op jit(solution)/shard_map/attend/pallas_call | solution.py:122
  8.2 7.5 %all-to-all-start = ((bf16[16,32,512]{2,1,0:T(8,128)(2,1)}), bf16[16,32,512]{2,1,0:T(8,128)(2,1)S(1)}, u32[]{:S(2)}, u32[]{:S(2)}) async-start(bf16[16,32,512]{2,1,0:T(8,128)(2,1)} %bitcast.26), calls=%async_computation | async-start | bytes 1048576 | tf_op jit(solution)/shard_map/all_to_all | solution.py:407
  15.7 0.1 pad_add_fusion.place
  15.8 5.2 %token_pieces.1 = (bf16[8,2,48,512]{3,2,1,0:T(8,128)(2,1)}, bf16[8,2,48,512]{3,2,1,0:T(8,128)(2,1)}) custom-call(s32[2]{0:T(128)S(1)} %pad_add_fusion.place, bf16[2,512,512]{2,1,0:T(8,128)(2,1)S(1)} %get-tuple-element.55.dscores, bf16[2,512,512]{2,1,0:T(8,128)(2,1)S(1)} %get-tuple-element.56.probs, bf16[2,512,48]{2,1,0:T(8,128)(2,1)} %get-tuple-element.57.refs_0_, ...), custom_call_target="tpu_custom_call" | custom-call | tf_op jit(solution)/shard_map/token_pieces/pallas_call | solution.py:172
  21.0 0.8 collective-permute-start.2
  21.8 2.6 %all-to-all-done.pieces = bf16[16,32,512]{2,1,0:T(8,128)(2,1)S(1)} async-done(((bf16[16,32,512]{2,1,0:T(8,128)(2,1)}), bf16[16,32,512]{2,1,0:T(8,128)(2,1)S(1)}, u32[]{:S(2)}, u32[]{:S(2)}) %all-to-all-start) | async-done | bytes 524320 | tf_op jit(solution)/shard_map/all_to_all | solution.py:407
  24.4 0.9 bias_rows_sum.1
  25.2 8.7 %all-to-all-start.1 = ((bf16[16,8,128]{2,1,0:T(8,128)(2,1)}), bf16[16,8,128]{2,1,0:T(8,128)(2,1)S(1)}, u32[]{:S(2)}, u32[]{:S(2)}) async-start(bf16[16,8,128]{2,1,0:T(8,128)(2,1)} %bias_rows_sum.1), calls=%async_computation.1 | async-start | bytes 65536 | tf_op jit(solution)/shard_map/all_to_all | solution.py:407
  33.9 3.5 %pair_forward_0.1 = (f32[1024,128]{1,0:T(8,128)}, f32[1024,128]{1,0:T(8,128)}, bf16[128,1024]{1,0:T(8,128)(2,1)}, bf16[256,1024]{1,0:T(8,128)(2,1)}, bf16[1024,2...) custom-call(bf16[1024,128]{1,0:T(8,128)(2,1)} %bitcast.33, bf16[2,128,256]{2,1,0:T(8,128)(2,1)} %refs_6_.1, ...), custom_call_target="tpu_custom_call" | custom-call | tf_op jit(solution)/shard_map/pair_forward_0/pallas_call | solution.py:277
  37.4 2.8 %pair_forward_1.1 = (f32[1024,128]{1,0:T(8,128)}, f32[1024,128]{1,0:T(8,128)}, bf16[128,1024]{1,0:T(8,128)(2,1)S(1)}, bf16[256,1024]{1,0:T(8,128)(2,1)S(1)}, bf1...) custom-call(f32[1024,128]{1,0:T(8,128)} %get-tuple-element.40.field_far, bf16[2,128,256]{2,1,0:T(8,128)(2,1)} %refs_6_.1, ...), custom_call_target="tpu_custom_call" | custom-call | tf_op jit(solution)/shard_map/pair_forward_1/pallas_call | solution.py:296
  40.2 2.3 %all-to-all-done.1.packed = bf16[16,8,128]{2,1,0:T(8,128)(2,1)S(1)} async-done(((bf16[16,8,128]{2,1,0:T(8,128)(2,1)}), bf16[16,8,128]{2,1,0:T(8,128)(2,1)S(1)}, u32[]{:S(2)}, u32[]{:S(2)}) %all-to-all-start.1) | async-done | bytes 32800 | tf_op jit(solution)/shard_map/all_to_all | solution.py:407
  42.5 0.0 copy-start
  42.5 5.7 %pair_backward.1 = (bf16[1024,128]{1,0:T(8,128)(2,1)}, bf16[16,3,16,128]{3,2,1,0:T(8,128)(2,1)S(1)}, bf16[16,3,16,128]{3,2,1,0:T(8,128)(2,1)S(1)}) custom-call(s32[1]{0:T(128)} %bitcast.core, bf16[16,8,128]{2,1,0:T(8,128)(2,1)S(1)} %all-to-all-done.1.packed, bf16[128,1024]{1,0:T(8,128)(2,1)S(1)} %get-tuple-element.41.refs_0_, ...), custom_call_target="tpu_custom_call" | custom-call | tf_op jit(solution)/shard_map/pair_backward/pallas_call | solution.py:389
  48.2 0.1 collective-permute-start
  48.3 1.4 %collective-permute-done = bf16[16,48,128]{2,1,0:T(8,128)(2,1)S(1)} collective-permute-done((bf16[16,48,128]{2,1,0:T(8,128)(2,1)S(1)}, bf16[16,48,128]{2,1,0:T(8,128)(2,1)S(1)}, u32[]{:S(2)}, u32[]{:S(2)}) %collective-permute-start) | collective-permute-done | bytes 196640 | tf_op jit(solution)/shard_map/ppermute | solution.py:415
  49.7 0.7 fusion
  50.4 7.1 %all-to-all-start.2 = ((bf16[16,48,128]{2,1,0:T(8,128)(2,1)}), bf16[16,48,128]{2,1,0:T(8,128)(2,1)S(1)}, u32[]{:S(2)}, u32[]{:S(2)}) async-start(bf16[16,48,128]{2,1,0:T(8,128)(2,1)} %fusion), calls=%async_computation.2 | async-start | bytes 393216 | tf_op jit(solution)/shard_map/all_to_all | solution.py:407
  57.5 0.0 collective-permute-done.2.received
  57.5 0.0 copy-done
  57.5 0.2 halve.3
  57.7 0.9 collective-permute-start.3
  58.6 5.8 %all-to-all-done.2 = bf16[16,48,128]{2,1,0:T(8,128)(2,1)S(1)} async-done(((bf16[16,48,128]{2,1,0:T(8,128)(2,1)}), bf16[16,48,128]{2,1,0:T(8,128)(2,1)S(1)}, u32[]{:S(2)}, u32[]{:S(2)}) %all-to-all-start.2) | async-done | bytes 196640 | tf_op jit(solution)/shard_map/all_to_all | solution.py:407
  64.5 15.6 %all_to_all.25 = bf16[8,48,128]{2,1,0:T(8,128)(2,1)S(1)} all-to-all(bf16[8,48,128]{2,1,0:T(8,128)(2,1)S(1)} %broadcast_in_dim.6), channel_id=1, replica_groups=mesh['yh'=2,'x'=4,'core'=2,'yl'=2,'z'=8] {'z'}, dimensions={0} | all-to-all | bytes 196608 | tf_op jit(solution)/shard_map/all_to_all | solution.py:407
  80.1 0.7 broadcast_in_dim.7
  80.8 5.2 %all-to-all-start.4 = ((bf16[16,48,128]{2,1,0:T(8,128)(2,1)}), bf16[16,48,128]{2,1,0:T(8,128)(2,1)S(1)}, u32[]{:S(2)}, u32[]{:S(2)}) async-start(bf16[16,48,128]{2,1,0:T(8,128)(2,1)} %broadcast_in_dim.7), calls=%async_computation.4 | async-start | bytes 393216 | tf_op jit(solution)/shard_map/all_to_all | solution.py:407
  86.0 0.0 collective-permute-done.3.received
  86.0 0.1 halve.4
  86.1 0.5 collective-permute-start.4
  86.6 6.0 %all-to-all-done.4 = bf16[16,48,128]{2,1,0:T(8,128)(2,1)S(1)} async-done(((bf16[16,48,128]{2,1,0:T(8,128)(2,1)}), bf16[16,48,128]{2,1,0:T(8,128)(2,1)S(1)}, u32[]{:S(2)}, u32[]{:S(2)}) %all-to-all-start.4) | async-done | bytes 196640 | tf_op jit(solution)/shard_map/all_to_all | solution.py:407
  92.6 0.0 collective-permute-start.1
  92.6 2.5 %collective-permute-done.4.received = bf16[2,2,48,512]{3,2,1,0:T(8,128)(2,1)S(1)} collective-permute-done((bf16[2,2,48,512]{3,2,1,0:T(8,128)(2,1)S(1)}, bf16[2,2,48,512]{3,2,1,0:T(8,128)(2,1)S(1)}, u32[]{:S(2)}, u32[]{:S(2)}) %collective-permute-start.4) | collective-permute-done | bytes 196640 | tf_op jit(solution)/shard_map/ppermute | solution.py:415
  95.2 0.9 collective-permute-start.5
  96.1 7.7 %collective-permute-done.5 = bf16[1,2,48,512]{3,2,1,0:T(8,128)(2,1)S(1)} collective-permute-done((bf16[1,2,48,512]{3,2,1,0:T(8,128)(2,1)S(1)}, bf16[1,2,48,512]{3,2,1,0:T(8,128)(2,1)S(1)}, u32[]{:S(2)}, u32[]{:S(2)}) %collective-permute-start.5) | collective-permute-done | bytes 98336 | tf_op jit(solution)/shard_map/ppermute | solution.py:415
  103.9 0.0 collective-permute-done.1
  103.9 1.0 finish.1
  (4 shorter events, 0.1 us)
Async XLA Ops:
  8.2 16.1 %all-to-all-start = ((bf16[16,32,512]{2,1,0:T(8,128)(2,1)}), bf16[16,32,512]{2,1,0:T(8,128)(2,1)S(1)}, u32[]{:S(2)}, u32[]{:S(2)}) async-start(bf16[16,32,512]{2,1,0:T(8,128)(2,1)} %bitcast.26), calls=%async_computation | async-start | bytes 1048576 | tf_op jit(solution)/shard_map/all_to_all | solution.py:407
  21.0 36.5 %collective-permute-start.2 = (bf16[8,2,48,512]{3,2,1,0:T(8,128)(2,1)}, bf16[8,2,48,512]{3,2,1,0:T(8,128)(2,1)S(1)}, u32[]{:S(2)}, u32[]{:S(2)}) collective-permute-start(bf16[8,2,48,512]{3,2,1,0:T(8,128)(2,1)} %get-tuple-element.61), channel_id=1, source_target_pairs={{0,8},{8,0},{1,9},{9,1},{2,10},{10,2},{3,11},{11,3},{4,12},{12,4},... | collective-permute-start | bytes 2359304 | tf_op jit(solution)/shard_map/ppermute | solution.py:415
  25.2 17.2 %all-to-all-start.1 = ((bf16[16,8,128]{2,1,0:T(8,128)(2,1)}), bf16[16,8,128]{2,1,0:T(8,128)(2,1)S(1)}, u32[]{:S(2)}, u32[]{:S(2)}) async-start(bf16[16,8,128]{2,1,0:T(8,128)(2,1)} %bias_rows_sum.1), calls=%async_computation.1 | async-start | bytes 65536 | tf_op jit(solution)/shard_map/all_to_all | solution.py:407
  42.5 15.1 %copy-start = (bf16[8,2,48,512]{3,2,1,0:T(8,128)(2,1)S(1)}, bf16[8,2,48,512]{3,2,1,0:T(8,128)(2,1)}, u32[]{:S(2)}) copy-start(bf16[8,2,48,512]{3,2,1,0:T(8,128)(2,1)} %get-tuple-element.60.kept) | copy-start | bytes 2359300
  48.2 1.5 %collective-permute-start = (bf16[16,48,128]{2,1,0:T(8,128)(2,1)S(1)}, bf16[16,48,128]{2,1,0:T(8,128)(2,1)S(1)}, u32[]{:S(2)}, u32[]{:S(2)}) collective-permute-start(bf16[16,48,128]{2,1,0:T(8,128)(2,1)S(1)} %bitcast.24), channel_id=1, source_target_pairs={{0,16},{16,0},{1,17},{17,1},{2,18},{18,2},{3,19},{19,3},{4,20},{20... | collective-permute-start | bytes 589832 | tf_op jit(solution)/shard_map/ppermute | solution.py:415
  50.4 14.0 %all-to-all-start.2 = ((bf16[16,48,128]{2,1,0:T(8,128)(2,1)}), bf16[16,48,128]{2,1,0:T(8,128)(2,1)S(1)}, u32[]{:S(2)}, u32[]{:S(2)}) async-start(bf16[16,48,128]{2,1,0:T(8,128)(2,1)} %fusion), calls=%async_computation.2 | async-start | bytes 393216 | tf_op jit(solution)/shard_map/all_to_all | solution.py:407
  57.7 28.3 %collective-permute-start.3 = (bf16[4,2,48,512]{3,2,1,0:T(8,128)(2,1)S(1)}, bf16[4,2,48,512]{3,2,1,0:T(8,128)(2,1)S(1)}, u32[]{:S(2)}, u32[]{:S(2)}) collective-permute-start(bf16[4,2,48,512]{3,2,1,0:T(8,128)(2,1)S(1)} %get-tuple-element.63), channel_id=1, source_target_pairs={{0,1},{1,0},{2,3},{3,2},{4,5},{5,4},{6,7},{7,6},{8,9},{9,8},{10,11... | collective-permute-start | bytes 1179656 | tf_op jit(solution)/shard_map/ppermute | solution.py:415
  80.8 11.8 %all-to-all-start.4 = ((bf16[16,48,128]{2,1,0:T(8,128)(2,1)}), bf16[16,48,128]{2,1,0:T(8,128)(2,1)S(1)}, u32[]{:S(2)}, u32[]{:S(2)}) async-start(bf16[16,48,128]{2,1,0:T(8,128)(2,1)} %broadcast_in_dim.7), calls=%async_computation.4 | async-start | bytes 393216 | tf_op jit(solution)/shard_map/all_to_all | solution.py:407
  86.1 9.0 %collective-permute-start.4 = (bf16[2,2,48,512]{3,2,1,0:T(8,128)(2,1)S(1)}, bf16[2,2,48,512]{3,2,1,0:T(8,128)(2,1)S(1)}, u32[]{:S(2)}, u32[]{:S(2)}) collective-permute-start(bf16[2,2,48,512]{3,2,1,0:T(8,128)(2,1)S(1)} %get-tuple-element.65), channel_id=1, source_target_pairs={{0,2},{1,3},{2,0},{3,1},{4,6},{5,7},{6,4},{7,5},{8,10},{9,11},{10,... | collective-permute-start | bytes 589832 | tf_op jit(solution)/shard_map/ppermute | solution.py:415
  92.6 11.2 %collective-permute-start.1 = (bf16[16,48,128]{2,1,0:T(8,128)(2,1)S(1)}, bf16[16,48,128]{2,1,0:T(8,128)(2,1)S(1)}, u32[]{:S(2)}, u32[]{:S(2)}) collective-permute-start(bf16[16,48,128]{2,1,0:T(8,128)(2,1)S(1)} %all-to-all-done.4), channel_id=1, source_target_pairs={{0,16},{16,0},{1,17},{17,1},{2,18},{18,2},{3,19},{19,3},{4,20},{20... | collective-permute-start | bytes 589832 | tf_op jit(solution)/shard_map/ppermute | solution.py:415
  95.2 8.7 %collective-permute-start.5 = (bf16[1,2,48,512]{3,2,1,0:T(8,128)(2,1)S(1)}, bf16[1,2,48,512]{3,2,1,0:T(8,128)(2,1)S(1)}, u32[]{:S(2)}, u32[]{:S(2)}) collective-permute-start(bf16[1,2,48,512]{3,2,1,0:T(8,128)(2,1)S(1)} %get-tuple-element.67), channel_id=1, source_target_pairs={{0,4},{1,5},{2,6},{3,7},{4,0},{5,1},{6,2},{7,3},{8,12},{9,13},{10,... | collective-permute-start | bytes 294920 | tf_op jit(solution)/shard_map/ppermute | solution.py:415
